TPU v7x, 256 devices: a whole 4x4x8 slice. The times are simulated.
256 devices in a mesh: seq: 32 (over y, z), mp: 8 (over x, core).
Axes of the slice: x: 4, y: 4, z: 8, core: 2. Of those that a mesh axis runs over, the one named last changes fastest.
Arguments:
- query_rows: bfloat16 [16384, 8192], P('seq', 'mp'), may hold values from -8 to 8
- key_rows: bfloat16 [16384, 1024], P('seq', 'mp'), may hold values from -8 to 8
- value_rows: bfloat16 [16384, 1024], P('seq', 'mp'), may hold values from -6 to 6
- cotangent: bfloat16 [16384, 8192], P('seq', 'mp'), may hold values from -6 to 6
- router_logits: float32 [16384], P('seq'), may hold values from -8 to 8
- selection: int32 [4096], P('seq'), may hold values from -1 to 511, as said below
Outputs:
- mixed: bfloat16 [16384, 8192], P('seq', 'mp')
- query_grad: bfloat16 [16384, 8192], P('seq', 'mp')
- key_grad: bfloat16 [16384, 1024], P('seq', 'mp')
- value_grad: bfloat16 [16384, 1024], P('seq', 'mp')
- router_grad: float32 [16384], P('seq')
Inputs may be any that keep to these rules, and one draw needn't show every extreme that they name: `selection`: each shard's block of 128 entries lists the local positions of its selected tokens in ascending order, then -1 in the remaining entries; all shards together select exactly 2048 tokens, and some shard selects exactly 128.
All inputs are finite; a program needn't handle non-finite values.
Results may differ from a plain program's by a relative error of at most 0.012.
The roundings to bfloat16 on the way count: a program that leaves them out, or rounds other values in their place, can miss the bound.
Values may be sent and summed in bfloat16 or wider, within the bound.
No kernel may reach another device: no remote copies, remote signals or barrier semaphores. Data moves between devices by JAX's collectives and lax.ppermute only.
A program may use at most 64 MiB of HBM per device.

v0:
```python
import jax
import jax.numpy as jnp
from jax import lax
from jax.sharding import PartitionSpec as P

HEAD_DIM = 128


def place_rows(values_in, targets, tok_rows):
    flat = values_in.reshape(-1, values_in.shape[-1])
    empty = jnp.zeros((tok_rows, flat.shape[-1]), flat.dtype)
    return empty.at[targets.reshape(-1)].set(flat, mode="drop")


def shards(query_rows, key_rows, value_rows, cotangent, router_logits, selection):
    axis_width = lax.axis_size("seq")
    shard_index = lax.axis_index("seq")
    tok_rows = query_rows.shape[0]
    slot_total = selection.shape[0]
    cap_slots = slot_total // axis_width
    block_rows = slot_total // 2
    q_cols = query_rows.shape[1]
    kv_cols = key_rows.shape[1]
    q_heads = q_cols // HEAD_DIM
    kv_heads_dev = kv_cols // HEAD_DIM
    group = q_heads // kv_heads_dev
    scale = HEAD_DIM ** (-0.5)
    picked = selection >= 0
    own_count = jnp.sum(picked.astype(jnp.int32))
    counts = lax.all_gather(own_count.reshape(1), "seq", axis=0, tiled=True)
    offsets = jnp.cumsum(counts) - counts
    lanes = jnp.arange(axis_width, dtype=jnp.int32)
    own_offset = jnp.sum(jnp.where(lanes == shard_index, offsets, 0))
    slot_steps = jnp.arange(cap_slots, dtype=jnp.int32)
    local_index = (
        jnp.mod(lanes - own_offset, axis_width)[:, None] + axis_width * slot_steps[None, :]
    )
    slot_live = local_index < own_count
    positions = jnp.where(slot_live, selection[local_index], tok_rows)
    safe_rows = jnp.minimum(positions, tok_rows - 1)
    live_mask = slot_live[:, :, None]
    router = jax.nn.sigmoid(router_logits[safe_rows])
    cot_rows = cotangent[safe_rows]
    query_send = jnp.where(live_mask, query_rows[safe_rows], 0)
    grad_send = jnp.where(live_mask, router[:, :, None] * cot_rows.astype(jnp.float32), 0.0).astype(
        jnp.bfloat16
    )
    query_recv, grad_recv = (
        lax.all_to_all(query_send, "seq", split_axis=0, concat_axis=0, tiled=True),
        lax.all_to_all(grad_send, "seq", split_axis=0, concat_axis=0, tiled=True),
    )
    row_ids = jnp.arange(block_rows, dtype=jnp.int32)
    query_rank = shard_index + axis_width * row_ids
    shard_ends = offsets + counts
    source = jnp.sum((shard_ends[None, :] <= query_rank[:, None]).astype(jnp.int32), axis=1)
    source_offset = offsets[source]
    first_rank = source_offset + jnp.mod(shard_index - source_offset, axis_width)
    slot_index = source * cap_slots + (query_rank - first_rank) // axis_width

    def compact(received):
        return received.reshape(axis_width * cap_slots, received.shape[2])[slot_index]

    own_rows = jnp.minimum(jnp.where(picked, selection, 0), tok_rows - 1)
    own_pairs = jnp.where(
        picked[:, None], jnp.concatenate([key_rows[own_rows], value_rows[own_rows]], axis=1), 0
    )
    key_set = lax.all_gather(own_pairs, "seq", axis=0, tiled=True)
    key_ids = jnp.arange(axis_width * slot_total, dtype=jnp.int32)
    key_source = key_ids // slot_total
    key_slot = jnp.mod(key_ids, slot_total)
    key_rank = jnp.where(
        key_slot < counts[key_source], offsets[key_source] + key_slot, axis_width * slot_total
    )
    query_block = compact(query_recv)
    grad_block = compact(grad_recv)
    allowed = key_rank[None, :] <= query_rank[:, None]
    contract = (((1,), (1,)), ((), ()))
    weight_list, dscore_list, output_list, dquery_list = ([], [], [], [])
    for head_index in range(q_heads):
        kv_head = head_index // group
        col_start = head_index * HEAD_DIM
        query_head = query_block[:, col_start : col_start + HEAD_DIM]
        grad_head = grad_block[:, col_start : col_start + HEAD_DIM]
        key_head = key_set[:, kv_head * HEAD_DIM : (kv_head + 1) * HEAD_DIM]
        value_head = key_set[:, kv_cols + kv_head * HEAD_DIM : kv_cols + (kv_head + 1) * HEAD_DIM]
        scores = (
            lax.dot_general(query_head, key_head, contract, preferred_element_type=jnp.float32)
            * scale
        )
        top_score = jnp.max(jnp.where(allowed, scores, -jnp.inf), axis=1, keepdims=True)
        expo = jnp.where(allowed, jnp.exp(scores - top_score), 0.0)
        weights = (expo / jnp.sum(expo, axis=1, keepdims=True)).astype(jnp.bfloat16)
        attended = jnp.dot(weights, value_head, preferred_element_type=jnp.float32).astype(
            jnp.bfloat16
        )
        slope = lax.dot_general(grad_head, value_head, contract, preferred_element_type=jnp.float32)
        centre = jnp.sum(
            grad_head.astype(jnp.float32) * attended.astype(jnp.float32), axis=1, keepdims=True
        )
        d_scores = (weights.astype(jnp.float32) * (slope - centre) * scale).astype(jnp.bfloat16)
        dquery_list.append(
            jnp.dot(d_scores, key_head, preferred_element_type=jnp.float32).astype(jnp.bfloat16)
        )
        weight_list.append(weights)
        dscore_list.append(d_scores)
        output_list.append(attended)
    attended_all = jnp.concatenate(output_list, axis=1)
    dquery_all = jnp.concatenate(dquery_list, axis=1)
    key_count = key_set.shape[0]
    weight_stack = jnp.stack(weight_list).reshape(kv_heads_dev, group, block_rows, key_count)
    dscore_stack = jnp.stack(dscore_list).reshape(kv_heads_dev, group, block_rows, key_count)
    query_split = query_block.reshape(block_rows, kv_heads_dev, group, HEAD_DIM)
    grad_split = grad_block.reshape(block_rows, kv_heads_dev, group, HEAD_DIM)
    back_first = offsets + jnp.mod(shard_index - offsets, axis_width)
    back_ranks = back_first[:, None] + axis_width * slot_steps[None, :]
    back_live = (back_ranks < shard_ends[:, None])[:, :, None]
    back_rows = jnp.minimum((back_ranks - shard_index) // axis_width, block_rows - 1)

    def slots_back(rows_in):
        return jnp.where(back_live, rows_in[back_rows], 0)

    key_part = jnp.einsum(
        "hgbk,bhgd->khd", dscore_stack, query_split, preferred_element_type=jnp.float32
    )
    value_part = jnp.einsum(
        "hgbk,bhgd->khd", weight_stack, grad_split, preferred_element_type=jnp.float32
    )
    pair_grads = lax.psum_scatter(
        jnp.concatenate(
            [
                key_part.reshape(lax.axis_size("seq") * slot_total, kv_cols),
                value_part.reshape(lax.axis_size("seq") * slot_total, kv_cols),
            ],
            axis=1,
        ),
        "seq",
        scatter_dimension=0,
        tiled=True,
    ).astype(jnp.bfloat16)
    out_back, dquery_back = (
        lax.all_to_all(slots_back(attended_all), "seq", split_axis=0, concat_axis=0, tiled=True),
        lax.all_to_all(slots_back(dquery_all), "seq", split_axis=0, concat_axis=0, tiled=True),
    )
    own_targets = jnp.where(picked, selection, tok_rows)
    key_grad = place_rows(pair_grads[:, :kv_cols], own_targets, tok_rows)
    value_grad = place_rows(pair_grads[:, kv_cols:], own_targets, tok_rows)
    out_float = out_back.astype(jnp.float32)
    mixed = place_rows((router[:, :, None] * out_float).astype(jnp.bfloat16), positions, tok_rows)
    query_grad = place_rows(dquery_back, positions, tok_rows)
    partial_sums = jnp.sum(cot_rows.astype(jnp.float32) * out_float, axis=2)
    feature_sum = lax.psum(partial_sums, "mp")
    router_terms = (router * (1.0 - router) * feature_sum).reshape(-1)
    router_grad = (
        jnp.zeros((tok_rows,), jnp.float32).at[positions.reshape(-1)].set(router_terms, mode="drop")
    )
    return (mixed, query_grad, key_grad, value_grad, router_grad)


def solution(mesh):
    in_specs = (P("seq", "mp"), P("seq", "mp"), P("seq", "mp"), P("seq", "mp"), P("seq"), P("seq"))
    out_specs = (P("seq", "mp"), P("seq", "mp"), P("seq", "mp"), P("seq", "mp"), P("seq"))
    return jax.shard_map(shards, mesh=mesh, in_specs=in_specs, out_specs=out_specs, check_vma=False)
```

profile of v0, /device:TPU:2, one launch (start us, length us, event | category | flops | bytes accessed | tf_op | source)
XLA Modules:
  0.0 416.4 jit_solution(17175785645465806378)
XLA Ops:
  7.2 1.9 compare_select_fusion.32
  16.4 23.8 %all-reduce = s32[32]{0:T(128)S(1)} all-reduce(s32[32]{0:T(128)S(1)} %dynamic-update-slice), channel_id=1, replica_groups=mesh['seq'=32,'mp'=8] {'seq'}, use_global_device_ids=true, to_apply=%add | all-reduce | flops 32 | bytes 256
  47.1 3.9 all-to-all-start
  54.6 4.4 %compare_select_fusion.21 = s32[4096,1]{0,1:T(1,128)S(1)} fusion(s32[]{:T(128)} %bitcast.62, s32[]{:T(128)} %bitcast.63, s32[]{:T(128)} %bitcast.64, s32[]{:T(128)} %bitcast.65, s32[]{:T(128)} %bitcast.66, s32[]{:T(128)} %bitcast.68, s32[]{:T(128)} %bitcast.67), kind=kLoop, calls=%fused_computation.197 | loop fusion | flops 94208 | bytes 16412 | tf_op jit(solution)/shard_map/gather | solution.py:72
  59.0 4.3 %compare_select_fusion.20 = s32[4096,1]{0,1:T(1,128)S(1)} fusion(s32[]{:T(128)} %bitcast.29, s32[]{:T(128)} %bitcast.30, s32[]{:T(128)} %bitcast.31, s32[]{:T(128)} %bitcast.32, s32[]{:T(128)} %bitcast.33, s32[]{:T(128)} %bitcast.35, s32[]{:T(128)} %bitcast.34), kind=kLoop, calls=%fused_computation.196 | loop fusion | flops 94208 | bytes 16412 | tf_op jit(solution)/shard_map/gather | solution.py:72
  65.3 31.4 %fusion.71 = s32[4096]{0:T(1024)S(1)} fusion(pred[4096]{0:T(1024)(128)(4,1)S(1)} %compare_reduce_fusion, pred[4096]{0:T(1024)(128)(4,1)S(1)} %compare_reduce_fusion.1, pred[4096]{0:T(1024)(128)(4,1)S(1)} %compare_reduce_fusion.2, pred[4096]{0:T(1024)(128)(4,1)S(1)} %compare_reduce_fusion.3, pred[4096]{0:T(1024)(128)(4,1)S(1)} %compare_reduce_fusion.4, ...), kind=kLoop, calls=%fused_computation.239 | loop fusion | flops 241664 | bytes 151752 | tf_op jit(solution)/shard_map/jit(_where)/select_n | solution.py:71
  97.6 1.9 convolution_multiply_fusion.1
  103.7 1.9 fusion.49
  119.2 1.9 broadcast_select_fusion.2
  121.1 9.9 %all-to-all-start.1 = ((bf16[32,4,1024]{2,1,0:T(4,128)(2,1)}), bf16[32,4,1024]{2,1,0:T(4,128)(2,1)}, u32[]{:S(2)}, u32[]{:S(2)}) async-start(bf16[32,4,1024]{2,1,0:T(4,128)(2,1)} %broadcast_select_fusion.2), calls=%async_computation.1 | async-start | bytes 524288 | tf_op jit(solution)/shard_map/all_to_all | solution.py:141
  132.4 3.1 gather_fusion.8
  135.5 1.9 reshape.887
  137.4 4.3 %all-to-all-done.1 = bf16[32,4,1024]{2,1,0:T(4,128)(2,1)} async-done(((bf16[32,4,1024]{2,1,0:T(4,128)(2,1)}), bf16[32,4,1024]{2,1,0:T(4,128)(2,1)}, u32[]{:S(2)}, u32[]{:S(2)}) %all-to-all-start.1) | async-done | bytes 262176 | tf_op jit(solution)/shard_map/all_to_all | solution.py:141
  141.8 2.9 fusion.51
  144.7 5.5 %all-to-all-start.2 = ((bf16[32,4,1024]{2,1,0:T(4,128)(2,1)}), bf16[32,4,1024]{2,1,0:T(4,128)(2,1)}, u32[]{:S(2)}, u32[]{:S(2)}) async-start(bf16[32,4,1024]{2,1,0:T(4,128)(2,1)} %get-tuple-element.50), calls=%async_computation.2 | async-start | bytes 524288 | tf_op jit(solution)/shard_map/all_to_all | solution.py:50
  151.1 9.8 %all-to-all-done.2 = bf16[32,4,1024]{2,1,0:T(4,128)(2,1)} async-done(((bf16[32,4,1024]{2,1,0:T(4,128)(2,1)}), bf16[32,4,1024]{2,1,0:T(4,128)(2,1)}, u32[]{:S(2)}, u32[]{:S(2)}) %all-to-all-start.2) | async-done | bytes 262176 | tf_op jit(solution)/shard_map/all_to_all | solution.py:50
  162.8 4.9 %convolution_bitcast_fusion = f32[4096,128]{0,1:T(8,128)S(1)} fusion(bf16[64,8,128]{2,1,0:T(8,128)(2,1)S(1)} %bitcast.167, bf16[8,64,4096]{2,1,0:T(8,128)(2,1)} %copy-done.4), kind=kOutput, calls=%fused_computation.32 | convolution fusion | flops 536870912 | bytes 6422528 | tf_op jit(solution)/shard_map/hgbk,bhgd->khd/dot_general | solution.py:125
  178.4 2.6 convolution_bitcast_fusion.1
  181.1 2.4 pad_maximum_fusion
  190.4 4.7 %all-to-all-start.3 = ((bf16[32,4,1024]{2,1,0:T(4,128)(2,1)}), bf16[32,4,1024]{2,1,0:T(4,128)(2,1)S(1)}, u32[]{:S(2)}, u32[]{:S(2)}) async-start(bf16[32,4,1024]{2,1,0:T(4,128)(2,1)} %broadcast_select_fusion.1), calls=%async_computation.3 | async-start | bytes 524288 | tf_op jit(solution)/shard_map/all_to_all | solution.py:142
  195.3 21.2 %psum.7 = f32[32,4]{1,0:T(8,128)S(1)} all-reduce(f32[32,4]{1,0:T(8,128)S(1)} %copy-done.31), channel_id=1, replica_groups=mesh['seq'=32,'mp'=8] {'mp'}, use_global_device_ids=true, to_apply=%region_34.35 | all-reduce | flops 128 | bytes 1024 | tf_op jit(solution)/shard_map/psum | solution.py:151
  216.7 2.2 scatter_custom_fusion
  220.5 2.2 scatter_custom_fusion.1
  222.7 182.4 %reduce-scatter.2.cloned.1.call-done = f32[128,256]{0,1:T(8,128)} async-done(((f32[4096,256]{0,1:T(8,128)}), f32[128,256]{0,1:T(8,128)}) %reduce-scatter.2.cloned.1.call-update) | async-done | bytes 131088 | tf_op jit(solution)/shard_map/reduce_scatter | solution.py:128
  (224 shorter events, 66.2 us)
Async XLA Ops:
  7.2 37.2 %copy-start = (bf16[512,1024]{1,0:T(8,128)(2,1)S(1)}, bf16[512,1024]{1,0:T(8,128)(2,1)}, u32[]{:S(2)}) copy-start(bf16[512,1024]{1,0:T(8,128)(2,1)} %param.6) | copy-start | bytes 3145732
  7.2 34.7 %copy-start.1 = (s32[128]{0:T(128)S(1)}, s32[128]{0:T(128)}, u32[]{:S(2)}) copy-start(s32[128]{0:T(128)} %param.11) | copy-start | bytes 1540
  7.2 90.3 %all-gather.2.cloned.1.call-start = ((), (), s32[]{:S(2)}) async-start(), calls=%async_computation.5 | async-start | bytes 2162688 | tf_op jit(solution)/shard_map/all_gather | solution.py:67
  47.1 49.6 %all-to-all-start = ((bf16[32,4,1024]{2,1,0:T(4,128)(2,1)}), bf16[32,4,1024]{2,1,0:T(4,128)(2,1)S(1)}, u32[]{:S(2)}, u32[]{:S(2)}) async-start(bf16[32,4,1024]{2,1,0:T(4,128)(2,1)} %broadcast_select_fusion), calls=%async_computation | async-start | bytes 524288 | tf_op jit(solution)/shard_map/all_to_all | solution.py:49
  107.6 5.5 %copy-start.13 = (bf16[64,4096]{1,0:T(8,128)(2,1)}, bf16[64,4096]{1,0:T(8,128)(2,1)S(1)}, u32[]{:S(2)}) copy-start(bf16[64,4096]{1,0:T(8,128)(2,1)S(1)} %get-tuple-element.34) | copy-start | bytes 1572868
  107.9 6.1 %copy-start.15 = (bf16[64,4096]{1,0:T(8,128)(2,1)}, bf16[64,4096]{1,0:T(8,128)(2,1)S(1)}, u32[]{:S(2)}) copy-start(bf16[64,4096]{1,0:T(8,128)(2,1)S(1)} %get-tuple-element.32) | copy-start | bytes 1572868
  108.2 6.7 %copy-start.17 = (bf16[64,4096]{1,0:T(8,128)(2,1)}, bf16[64,4096]{1,0:T(8,128)(2,1)S(1)}, u32[]{:S(2)}) copy-start(bf16[64,4096]{1,0:T(8,128)(2,1)S(1)} %get-tuple-element.30) | copy-start | bytes 1572868
  115.9 15.1 %copy-start.2 = (f32[512]{0:T(512)S(1)}, f32[512]{0:T(512)}, u32[]{:S(2)}) copy-start(f32[512]{0:T(512)} %param.10) | copy-start | bytes 6148
  121.1 20.7 %all-to-all-start.1 = ((bf16[32,4,1024]{2,1,0:T(4,128)(2,1)}), bf16[32,4,1024]{2,1,0:T(4,128)(2,1)}, u32[]{:S(2)}, u32[]{:S(2)}) async-start(bf16[32,4,1024]{2,1,0:T(4,128)(2,1)} %broadcast_select_fusion.2), calls=%async_computation.1 | async-start | bytes 524288 | tf_op jit(solution)/shard_map/all_to_all | solution.py:141
  132.4 12.3 %copy-start.29 = (f32[32,4]{1,0:T(8,128)}, f32[32,4]{1,0:T(8,128)S(1)}, u32[]{:S(2)}) copy-start(f32[32,4]{1,0:T(8,128)S(1)} %reshape.969) | copy-start | bytes 1540
  144.7 16.3 %all-to-all-start.2 = ((bf16[32,4,1024]{2,1,0:T(4,128)(2,1)}), bf16[32,4,1024]{2,1,0:T(4,128)(2,1)}, u32[]{:S(2)}, u32[]{:S(2)}) async-start(bf16[32,4,1024]{2,1,0:T(4,128)(2,1)} %get-tuple-element.50), calls=%async_computation.2 | async-start | bytes 524288 | tf_op jit(solution)/shard_map/all_to_all | solution.py:50
  150.2 254.9 %reduce-scatter.2.cloned.1.call-start = ((), (), s32[]{:S(2)}) async-start(), calls=%async_computation.6 | async-start | bytes 4325376 | tf_op jit(solution)/shard_map/reduce_scatter | solution.py:128
  162.7 5.0 %copy-start.32 = (bf16[64,128]{1,0:T(8,128)(2,1)S(1)}, bf16[64,128]{1,0:T(8,128)(2,1)}, u32[]{:S(2)}) copy-start(bf16[64,128]{1,0:T(8,128)(2,1)} %get-tuple-element.125) | copy-start | bytes 49156
  162.7 5.0 %copy-start.33 = (bf16[64,128]{1,0:T(8,128)(2,1)S(1)}, bf16[64,128]{1,0:T(8,128)(2,1)}, u32[]{:S(2)}) copy-start(bf16[64,128]{1,0:T(8,128)(2,1)} %get-tuple-element.127) | copy-start | bytes 49156
  162.7 5.0 %copy-start.34 = (bf16[64,128]{1,0:T(8,128)(2,1)S(1)}, bf16[64,128]{1,0:T(8,128)(2,1)}, u32[]{:S(2)}) copy-start(bf16[64,128]{1,0:T(8,128)(2,1)} %get-tuple-element.129) | copy-start | bytes 49156
  162.7 5.0 %copy-start.35 = (bf16[64,128]{1,0:T(8,128)(2,1)S(1)}, bf16[64,128]{1,0:T(8,128)(2,1)}, u32[]{:S(2)}) copy-start(bf16[64,128]{1,0:T(8,128)(2,1)} %get-tuple-element.131) | copy-start | bytes 49156
  162.7 5.0 %copy-start.36 = (bf16[64,128]{1,0:T(8,128)(2,1)S(1)}, bf16[64,128]{1,0:T(8,128)(2,1)}, u32[]{:S(2)}) copy-start(bf16[64,128]{1,0:T(8,128)(2,1)} %get-tuple-element.133) | copy-start | bytes 49156
  162.7 5.0 %copy-start.37 = (bf16[64,128]{1,0:T(8,128)(2,1)S(1)}, bf16[64,128]{1,0:T(8,128)(2,1)}, u32[]{:S(2)}) copy-start(bf16[64,128]{1,0:T(8,128)(2,1)} %get-tuple-element.135) | copy-start | bytes 49156
  162.8 5.0 %copy-start.38 = (bf16[64,128]{1,0:T(8,128)(2,1)S(1)}, bf16[64,128]{1,0:T(8,128)(2,1)}, u32[]{:S(2)}) copy-start(bf16[64,128]{1,0:T(8,128)(2,1)} %get-tuple-element.137) | copy-start | bytes 49156
  162.8 5.2 %copy-start.22 = (bf16[64,4096]{1,0:T(8,128)(2,1)S(1)}, bf16[64,4096]{1,0:T(8,128)(2,1)}, u32[]{:S(2)}) copy-start(bf16[64,4096]{1,0:T(8,128)(2,1)} %copy-done.21) | copy-start | bytes 1572868
  188.5 6.8 %copy-start.19 = (bf16[32,4,1024]{2,1,0:T(4,128)(2,1)S(1)}, bf16[32,4,1024]{2,1,0:T(4,128)(2,1)}, u32[]{:S(2)}) copy-start(bf16[32,4,1024]{2,1,0:T(4,128)(2,1)} %get-tuple-element.51) | copy-start | bytes 786436
  188.5 6.9 %copy-start.31 = (f32[32,4]{1,0:T(8,128)S(1)}, f32[32,4]{1,0:T(8,128)}, u32[]{:S(2)}) copy-start(f32[32,4]{1,0:T(8,128)} %get-tuple-element.49) | copy-start | bytes 1540
  188.5 28.1 %copy-start.30 = (f32[32,4]{1,0:T(8,128)S(1)}, f32[32,4]{1,0:T(8,128)}, u32[]{:S(2)}) copy-start(f32[32,4]{1,0:T(8,128)} %copy-done.29) | copy-start | bytes 1540
  190.4 30.0 %all-to-all-start.3 = ((bf16[32,4,1024]{2,1,0:T(4,128)(2,1)}), bf16[32,4,1024]{2,1,0:T(4,128)(2,1)S(1)}, u32[]{:S(2)}, u32[]{:S(2)}) async-start(bf16[32,4,1024]{2,1,0:T(4,128)(2,1)} %broadcast_select_fusion.1), calls=%async_computation.3 | async-start | bytes 524288 | tf_op jit(solution)/shard_map/all_to_all | solution.py:142
  (22 other events, 59.8 us)
Sparse Core Ops, SparseCore 0:
  13.8 81.9 all-gather.1
  183.6 221.4 reduce-scatter.1
where the time goes:
time: 418 us; the launch traced here: 416 us
  waiting for transfers between devices  197 us (47%)
  other arithmetic  62.7 us (15%)
  blocking collectives  45 us (11%)
  local copies, waits for them, and re-layouts  36.6 us (9%)
  matrix products  36.3 us (9%)
  starting transfers between devices  24.2 us (6%)
  between operations  14.9 us (4%)
    reduce_scatter x1, waiting for transfers between devices, shards(): lax.psum_scatter(jnp.concatenate([key_part.reshape(lax.axis_size('seq') *...  182 us
    select_n x1, other arithmetic, shards(): jnp.where(key_slot < counts[key_source], offsets[key_source] + key_slot,...  31.4 us
    unnamed x1, blocking collectives  23.8 us
    psum x1, blocking collectives, shards(): feature_sum = lax.psum(partial_sums, 'mp')  21.2 us
    dot_general x8, matrix products, shards(): lax.dot_general(grad_head, value_head, contract, preferred_element_type=j...  10.3 us
    all_to_all x1, starting transfers between devices, shards(): lax.all_to_all(slots_back(attended_all), 'seq', split_axis=0, concat_axis...  9.91 us
    all_to_all x1, waiting for transfers between devices, shards(): lax.all_to_all(grad_send, 'seq', split_axis=0, concat_axis=0, tiled=True)  9.83 us
  transfers between devices with their start and end apart: 6, of which 3 were waited for; matrix products, arithmetic and copies ran while one was open for 18% of the time, Pallas kernels for 0%

commit v1 on v0

v1 whole, which is shorter than its diff:
```python
import functools

import jax
import jax.numpy as jnp
from jax import lax
from jax.experimental import pallas as pl
from jax.experimental.pallas import tpu as pltpu
from jax.sharding import Mesh, PartitionSpec as P

HEAD_DIM = 128
SLOTS = 128
TOK = 512
HEADS = 8
ROWS_Y = 4
ROWS_Z = 8
LANES = HEADS * HEAD_DIM
KEYS = ROWS_Y * ROWS_Z * SLOTS
TILE = 256
QCHUNK = 256
FLAG = 64.0
NEG = -1e30
SCALE = HEAD_DIM ** (-0.5)
LOG2E = 1.4426950408889634
BF = jnp.bfloat16
F32 = jnp.float32
NT = (((1,), (1,)), ((), ()))
NN = (((1,), (0,)), ((), ()))
VMEM = pltpu.VMEM
LIMIT = 60 * 1024 * 1024


def dot(a, b, dims=NN):
    return lax.dot_general(a, b, dims, preferred_element_type=F32)


def column_of(row):
    return jnp.transpose(jnp.broadcast_to(row, (SLOTS, SLOTS)))


def picker(sel_row):
    col = column_of(sel_row.astype(F32))
    lane = lax.broadcasted_iota(jnp.int32, (SLOTS, SLOTS), 1).astype(F32)
    return jnp.concatenate([col == lane + float(c * SLOTS) for c in range(TOK // SLOTS)], axis=1)


def placer(sel_row):
    token = lax.broadcasted_iota(jnp.int32, (TOK, SLOTS), 0)
    return jnp.broadcast_to(sel_row, (TOK, SLOTS)) == token


def one_hot(mask):
    return jnp.where(mask, 1.0, 0.0).astype(BF)


def select_kv_kernel(sel_ref, key_ref, value_ref, out_ref):
    sel = sel_ref[...]
    pick = one_hot(picker(sel))
    live = column_of(sel.astype(F32)) >= 0.0
    key = jnp.where(live, dot(pick, key_ref[...]), FLAG).astype(BF)
    value = dot(pick, value_ref[...]).astype(BF)
    for copy in range(ROWS_Z):
        out_ref[copy, :, :HEAD_DIM] = key
        out_ref[copy, :, HEAD_DIM:] = value


def select_q_kernel(sel_ref, logit_ref, query_ref, cot_ref, q_ref, g_ref, c_ref, router_ref):
    mask = picker(sel_ref[...])
    pick = one_hot(mask)
    logit = jnp.sum(jnp.where(mask, logit_ref[...], 0.0), axis=1, keepdims=True)
    router = 1.0 / (1.0 + jnp.exp(-logit))
    router_ref[...] = jnp.broadcast_to(router, (SLOTS, SLOTS))
    for h in range(HEADS):
        cols = slice(h * HEAD_DIM, (h + 1) * HEAD_DIM)
        rows = slice(h * SLOTS, (h + 1) * SLOTS)
        q_ref[rows, :] = dot(pick, query_ref[:, cols]).astype(BF)
        cot = dot(pick, cot_ref[:, cols])
        c_ref[rows, :] = cot.astype(BF)
        g_ref[rows, :] = (router * cot).astype(BF)


def attention_kernel(pos_ref, kv0, kv1, kv2, kv3, q_ref, g_ref, c_ref,
                     att_ref, dq_ref, dkv_ref, feat_ref,
                     kvs, s_ref, w_ref, at_ref, dqt_ref, top_ref, sum_ref, cen_ref, sem):
    row = pos_ref[0]
    col = pos_ref[1]
    block = ROWS_Z * SLOTS
    copies = []
    for k, src in enumerate((kv0, kv1, kv2, kv3)):
        owner = lax.rem(row - k + ROWS_Y, ROWS_Y)
        start = pl.multiple_of(owner * block, block)
        copies.append(pltpu.make_async_copy(src, kvs.at[pl.ds(start, block), :], sem.at[k]))
    for c in copies:
        c.start()
    at_ref[...] = jnp.zeros_like(at_ref)
    dqt_ref[...] = jnp.zeros_like(dqt_ref)
    top_ref[...] = jnp.full_like(top_ref, NEG)
    sum_ref[...] = jnp.zeros_like(sum_ref)
    tiles = row * (block // TILE) + col * SLOTS // TILE + 1
    query_id = (row * ROWS_Z + col) * SLOTS
    for c in copies:
        c.wait()

    def scores(t, carry):
        keys = kvs[pl.ds(pl.multiple_of(t * TILE, TILE), TILE), :HEAD_DIM]
        kid = t * TILE + lax.broadcasted_iota(jnp.int32, (TILE, SLOTS), 0)
        qid = query_id + lax.broadcasted_iota(jnp.int32, (TILE, SLOTS), 1)
        dead = jnp.broadcast_to(keys[:, :1].astype(F32), (TILE, SLOTS)) > 0.5 * FLAG
        bias = jnp.where((kid > qid) | dead, NEG, 0.0)
        bias = jnp.concatenate([bias] * (QCHUNK // SLOTS), axis=1)
        for c in range(LANES // QCHUNK):
            lanes = slice(c * QCHUNK, (c + 1) * QCHUNK)
            s = dot(keys, q_ref[lanes, :], NT) * (SCALE * LOG2E) + bias
            s_ref[pl.ds(pl.multiple_of(t * TILE, TILE), TILE), lanes] = s
            part = jnp.max(s.reshape(TILE // 8, 8, QCHUNK), axis=0)
            top_ref[:, lanes] = jnp.maximum(top_ref[:, lanes], part)
        return carry

    lax.fori_loop(0, tiles, scores, 0)
    top_ref[...] = jnp.broadcast_to(jnp.max(top_ref[...], axis=0, keepdims=True), top_ref.shape)

    def exponent(t, carry):
        rows = pl.ds(pl.multiple_of(t * TILE, TILE), TILE)
        for c in range(LANES // QCHUNK):
            lanes = slice(c * QCHUNK, (c + 1) * QCHUNK)
            e = jnp.exp2(s_ref[rows, lanes] - top_ref[:1, lanes])
            s_ref[rows, lanes] = e
            sum_ref[:, lanes] += jnp.sum(e.reshape(TILE // 8, 8, QCHUNK), axis=0)
        return carry

    lax.fori_loop(0, tiles, exponent, 0)
    total = jnp.sum(sum_ref[...], axis=0, keepdims=True)
    sum_ref[...] = jnp.broadcast_to(1.0 / total, sum_ref.shape)

    def forward(t, carry):
        rows = pl.ds(pl.multiple_of(t * TILE, TILE), TILE)
        value_t = jnp.transpose(kvs[rows, HEAD_DIM:])
        for c in range(LANES // QCHUNK):
            lanes = slice(c * QCHUNK, (c + 1) * QCHUNK)
            w = (s_ref[rows, lanes] * sum_ref[:1, lanes]).astype(BF)
            w_ref[rows, lanes] = w
            at_ref[:, lanes] += dot(value_t, w)
        dkv_ref[rows, HEAD_DIM:] = dot(w_ref[rows, :], g_ref[...]).astype(BF)
        return carry

    lax.fori_loop(0, tiles, forward, 0)

    feature = jnp.zeros((SLOTS, HEAD_DIM), F32)
    for h in range(HEADS):
        lanes = slice(h * HEAD_DIM, (h + 1) * HEAD_DIM)
        att_t = at_ref[:, lanes].astype(BF)
        att = jnp.transpose(att_t)
        att_ref[:, lanes] = att
        grad_t = jnp.transpose(g_ref[lanes, :])
        centre = jnp.sum(grad_t.astype(F32) * att_t.astype(F32), axis=0, keepdims=True)
        cen_ref[:, lanes] = jnp.broadcast_to(centre, (8, HEAD_DIM))
        feature += c_ref[lanes, :].astype(F32) * att.astype(F32)
    feature = jnp.broadcast_to(jnp.sum(feature, axis=1, keepdims=True), (SLOTS, SLOTS))
    feature = jnp.transpose(feature)[:8, :]
    for peer in range(8):
        feat_ref[peer] = feature

    def backward(t, carry):
        rows = pl.ds(pl.multiple_of(t * TILE, TILE), TILE)
        values = kvs[rows, HEAD_DIM:]
        key_t = jnp.transpose(kvs[rows, :HEAD_DIM])
        acc = jnp.zeros((TILE, HEAD_DIM), F32)
        for c in range(LANES // QCHUNK):
            lanes = slice(c * QCHUNK, (c + 1) * QCHUNK)
            slope = dot(values, g_ref[lanes, :], NT)
            ds = (w_ref[rows, lanes].astype(F32) * (slope - cen_ref[:1, lanes]) * SCALE).astype(BF)
            dqt_ref[:, lanes] += dot(key_t, ds)
            acc += dot(ds, q_ref[lanes, :])
        dkv_ref[rows, :HEAD_DIM] = acc.astype(BF)
        return carry

    lax.fori_loop(0, tiles, backward, 0)

    def clear(t, carry):
        dkv_ref[pl.ds(pl.multiple_of(t * TILE, TILE), TILE), :] = jnp.zeros((TILE, 2 * HEAD_DIM), BF)
        return carry

    lax.fori_loop(tiles, KEYS // TILE, clear, 0)
    for h in range(HEADS):
        lanes = slice(h * HEAD_DIM, (h + 1) * HEAD_DIM)
        dq_ref[:, lanes] = jnp.transpose(dqt_ref[:, lanes].astype(BF))


def place_q_kernel(sel_ref, router_ref, att_ref, dq_ref, mixed_ref, qgrad_ref):
    place = one_hot(placer(sel_ref[...]))
    router = router_ref[...]
    for h in range(HEADS):
        lanes = slice(h * HEAD_DIM, (h + 1) * HEAD_DIM)
        mix = (router * att_ref[:, lanes].astype(F32)).astype(BF)
        mixed_ref[:, lanes] = dot(place, mix).astype(BF)
        qgrad_ref[:, lanes] = dot(place, dq_ref[:, lanes]).astype(BF)


def add_rows_kernel(in_ref, out_ref):
    total = in_ref[0].astype(F32)
    for k in range(1, ROWS_Y):
        total += in_ref[k].astype(F32)
    out_ref[...] = total.astype(BF)


def place_kv_kernel(sel_ref, router_ref, feat_ref, part_ref, kgrad_ref, vgrad_ref, rgrad_ref):
    total = part_ref[0].astype(F32)
    for k in range(1, ROWS_Z):
        total += part_ref[k].astype(F32)
    placed = dot(one_hot(placer(sel_ref[...])), total.astype(BF)).astype(BF)
    kgrad_ref[...] = placed[:, :HEAD_DIM]
    vgrad_ref[...] = placed[:, HEAD_DIM:]
    feature = feat_ref[0]
    for k in range(1, 8):
        feature += feat_ref[k]
    router = router_ref[...]
    terms = router * (1.0 - router) * column_of(feature[:1, :])
    terms = jnp.concatenate([terms] * (TOK // SLOTS), axis=1)
    rgrad_ref[...] = jnp.sum(jnp.where(picker(sel_ref[...]), terms, 0.0), axis=0, keepdims=True)


def call(kernel, outs, args, scratch=(), specs=None, cost=None):
    return pl.pallas_call(
        kernel,
        out_shape=[jax.ShapeDtypeStruct(s, d) for s, d in outs],
        in_specs=specs or [pl.BlockSpec(memory_space=VMEM)] * len(args),
        out_specs=[pl.BlockSpec(memory_space=VMEM)] * len(outs),
        scratch_shapes=list(scratch),
        compiler_params=pltpu.CompilerParams(vmem_limit_bytes=LIMIT if scratch else 24 * 1024 * 1024),
        cost_estimate=pl.CostEstimate(flops=cost[0], bytes_accessed=cost[1], transcendentals=0),
    )(*args)


def shards(query_rows, key_rows, value_rows, cotangent, router_logits, selection):
    sel = selection.reshape(1, SLOTS)
    logits = router_logits.reshape(1, TOK)
    row = lax.axis_index("y")
    col = lax.axis_index("z")
    (own,) = call(select_kv_kernel, [((ROWS_Z, SLOTS, 2 * HEAD_DIM), BF)], (sel, key_rows, value_rows),
                  cost=(2 * SLOTS * TOK * 256, 1 << 20))
    line = lax.all_to_all(own, "z", 0, 0, tiled=True)
    q, g, c, router = call(
        select_q_kernel,
        [((LANES, HEAD_DIM), BF)] * 3 + [((SLOTS, SLOTS), F32)],
        (sel, logits, query_rows, cotangent),
        cost=(4 * SLOTS * TOK * LANES, 3 << 20))
    line = line.reshape(ROWS_Z * SLOTS, 2 * HEAD_DIM)
    lines = [line] + [
        lax.ppermute(line, "y", [(s, (s + k) % ROWS_Y) for s in range(ROWS_Y)]) for k in range(1, ROWS_Y)
    ]
    pos = jnp.stack([row, col]).astype(jnp.int32)
    specs = [pl.BlockSpec(memory_space=pltpu.SMEM)] + [pl.BlockSpec(memory_space=pl.ANY)] * 4
    specs += [pl.BlockSpec(memory_space=VMEM)] * 3
    att, dq, dkv, feat = call(
        attention_kernel,
        [((SLOTS, LANES), BF), ((SLOTS, LANES), BF), ((KEYS, 2 * HEAD_DIM), BF), ((8, 8, SLOTS), F32)],
        (pos, *lines, q, g, c),
        scratch=[
            VMEM((KEYS, 2 * HEAD_DIM), BF), VMEM((KEYS, LANES), F32), VMEM((KEYS, LANES), BF),
            VMEM((HEAD_DIM, LANES), F32), VMEM((HEAD_DIM, LANES), F32),
            VMEM((8, LANES), F32), VMEM((8, LANES), F32), VMEM((8, LANES), F32),
            pltpu.SemaphoreType.DMA((4,)),
        ],
        specs=specs,
        cost=(12 * KEYS * LANES * HEAD_DIM, 8 << 20))
    feat = lax.all_to_all(feat, "mp", 0, 0, tiled=True)
    part = lax.all_to_all(dkv.reshape(ROWS_Y, ROWS_Z * SLOTS, 2 * HEAD_DIM), "y", 0, 0, tiled=True)
    mixed, qgrad = call(place_q_kernel, [((TOK, LANES), BF)] * 2, (sel, router, att, dq),
                        cost=(4 * SLOTS * TOK * LANES, 3 << 20))
    (part,) = call(add_rows_kernel, [((ROWS_Z * SLOTS, 2 * HEAD_DIM), BF)], (part,),
                   cost=(1 << 20, 3 << 20))
    part = lax.all_to_all(part.reshape(ROWS_Z, SLOTS, 2 * HEAD_DIM), "z", 0, 0, tiled=True)
    kgrad, vgrad, rgrad = call(
        place_kv_kernel,
        [((TOK, HEAD_DIM), BF)] * 2 + [((1, TOK), F32)],
        (sel, router, feat, part),
        cost=(2 * SLOTS * TOK * 256, 1 << 20))
    return mixed, qgrad, kgrad, vgrad, rgrad.reshape(TOK)


def solution(mesh):
    inner = Mesh(mesh.devices.reshape(ROWS_Y, ROWS_Z, 8), ("y", "z", "mp"))
    seq = ("y", "z")
    in_specs = (P(seq, "mp"), P(seq, "mp"), P(seq, "mp"), P(seq, "mp"), P(seq), P(seq))
    out_specs = (P(seq, "mp"), P(seq, "mp"), P(seq, "mp"), P(seq, "mp"), P(seq))
    return jax.shard_map(shards, mesh=inner, in_specs=in_specs, out_specs=out_specs, check_vma=False)
```

time: 418 us -> 152 us (0.36)
  waiting for transfers between devices: 197 us -> 35.1 us
  other arithmetic: 62.7 us -> 0.58 us
  matrix products: 36.3 us -> 0 us
  blocking collectives: 45 us -> 75.2 us
  local copies, waits for them, and re-layouts: 36.6 us -> 8 us
  between operations: 14.9 us -> 0.72 us
  Pallas kernels: 0 us -> 11.7 us
  starting transfers between devices: 24.2 us -> 17.9 us
    reduce_scatter x1 -> x0, waiting for transfers between devices: 182 us -> none  [shards(): lax.psum_scatter(jnp.concatenate([key_part.reshape(lax.axis_size('seq') *...]
    all_to_all x0 -> x2, blocking collectives: none -> 75.2 us  [the longest x1 49.4 us: shards(): lax.all_to_all(dkv.reshape(ROWS_Y, ROWS_Z * SLOTS, 2 * HEAD_DIM), 'y', 0,...]
    select_n x13 -> x0, other arithmetic: 39.9 us -> none  [the longest x1 31.4 us: shards(): jnp.where(key_slot < counts[key_source], offsets[key_source] + key_slot,...]
    dot_general x34 -> x0, matrix products: 36.3 us -> none  [the longest x8 10.3 us: shards(): lax.dot_general(grad_head, value_head, contract, preferred_element_type=j...]
    unnamed x1 -> x0, blocking collectives: 23.8 us -> none
    psum x1 -> x0, blocking collectives: 21.2 us -> none  [shards(): feature_sum = lax.psum(partial_sums, 'mp')]
    gather x21 -> x0, local copies, waits for them, and re-layouts: 19.3 us -> none  [the longest x4 4.29 us: slots_back(): return jnp.where(back_live, rows_in[back_rows], 0)]
    ppermute x0 -> x3, waiting for transfers between devices: none -> 16.8 us  [shards(): lax.ppermute(line, 'y', [(s, (s + k) % ROWS_Y) for s in range(ROWS_Y)])]
  transfers between devices with their start and end apart: 6 -> 5, of which waited for: 3 -> 4; matrix products, arithmetic and copies ran while one was open for 18% -> 0% of each run, Pallas kernels for 0% -> 3%
where the time goes in v1:
time: 152 us; the launch traced here: 149 us
  blocking collectives  75.2 us (49%)
  waiting for transfers between devices  35.1 us (23%)
  starting transfers between devices  17.9 us (12%)
  Pallas kernels  11.7 us (8%)
  local copies, waits for them, and re-layouts  8 us (5%)
    all_to_all x1, blocking collectives, shards(): lax.all_to_all(dkv.reshape(ROWS_Y, ROWS_Z * SLOTS, 2 * HEAD_DIM), 'y', 0,...  49.4 us
    all_to_all x1, blocking collectives, shards(): line = lax.all_to_all(own, 'z', 0, 0, tiled=True)  25.8 us
    ppermute x3, waiting for transfers between devices, shards(): lax.ppermute(line, 'y', [(s, (s + k) % ROWS_Y) for s in range(ROWS_Y)])  16.8 us
    all_to_all x1, waiting for transfers between devices, shards(): lax.all_to_all(part.reshape(ROWS_Z, SLOTS, 2 * HEAD_DIM), 'z', 0, 0, tile...  15.3 us
    pallas_call x6, Pallas kernels, call(): pl.pallas_call(kernel, out_shape=[jax.ShapeDtypeStruct(s, d) for s, d in...  11.7 us
    all_to_all x1, starting transfers between devices, shards(): lax.all_to_all(part.reshape(ROWS_Z, SLOTS, 2 * HEAD_DIM), 'z', 0, 0, tile...  8.38 us
    unnamed x34, local copies, waits for them, and re-layouts  8 us
    all_to_all x1, starting transfers between devices, shards(): feat = lax.all_to_all(feat, 'mp', 0, 0, tiled=True)  4.96 us
  transfers between devices with their start and end apart: 5, of which 4 were waited for; matrix products, arithmetic and copies ran while one was open for 0% of the time, Pallas kernels for 3%

profile of v1, /device:TPU:2, one launch (start us, length us, event | category | flops | bytes accessed | tf_op | source)
XLA Modules:
  0.0 149.2 jit_solution(11718397985615717037)
XLA Ops:
  0.7 1.0 copy-done.2
  1.6 0.9 copy-done.3
  2.5 0.7 copy-done.4
  3.5 25.8 %all_to_all.20 = bf16[8,128,256]{2,1,0:T(8,128)(2,1)S(1)} all-to-all(bf16[8,128,256]{2,1,0:T(8,128)(2,1)S(1)} %shard_map.102), channel_id=1, replica_groups=mesh['y'=4,'z'=8,'mp'=8] {'z'}, dimensions={0} | all-to-all | bytes 1048576 | tf_op jit(solution)/shard_map/all_to_all | solution.py:240
  29.2 3.0 %collective-permute-start.2 = (bf16[1024,256]{1,0:T(8,128)(2,1)S(1)}, bf16[1024,256]{1,0:T(8,128)(2,1)S(1)}, u32[]{:S(2)}, u32[]{:S(2)}) collective-permute-start(bf16[1024,256]{1,0:T(8,128)(2,1)S(1)} %bitcast.14), channel_id=1, source_target_pairs={{0,192},{64,0},{128,64},{192,128},{1,193},{65,1},{129,65},{193,129... | collective-permute-start | bytes 1572872 | tf_op jit(solution)/shard_map/ppermute | solution.py:248
  32.9 1.0 collective-permute-start
  33.9 1.2 copy-done.1
  35.7 0.7 copy-done.7
  36.4 0.8 shard_map.101
  37.2 0.7 copy-done.8
  37.9 0.7 copy-done.9
  38.6 0.7 copy-done.10
  39.9 13.1 %collective-permute-done.2.kv3 = bf16[1024,256]{1,0:T(8,128)(2,1)S(1)} collective-permute-done((bf16[1024,256]{1,0:T(8,128)(2,1)S(1)}, bf16[1024,256]{1,0:T(8,128)(2,1)S(1)}, u32[]{:S(2)}, u32[]{:S(2)}) %collective-permute-start.2) | collective-permute-done | bytes 524320 | tf_op jit(solution)/shard_map/ppermute | solution.py:248
  53.0 3.7 %collective-permute-done.kv1 = bf16[1024,256]{1,0:T(8,128)(2,1)S(1)} collective-permute-done((bf16[1024,256]{1,0:T(8,128)(2,1)S(1)}, bf16[1024,256]{1,0:T(8,128)(2,1)S(1)}, u32[]{:S(2)}, u32[]{:S(2)}) %collective-permute-start) | collective-permute-done | bytes 524320 | tf_op jit(solution)/shard_map/ppermute | solution.py:248
  56.7 0.8 copy-done.16
  57.5 6.6 %shard_map.103 = (bf16[128,1024]{1,0:T(8,128)(2,1)}, bf16[128,1024]{1,0:T(8,128)(2,1)}, bf16[4096,256]{1,0:T(8,128)(2,1)}, f32[8,8,128]{2,1,0:T(8,128)}) custom-call(s32[2]{0:T(128)} %pad_add_fusion.pos_ref, bf16[1024,256]{1,0:T(8,128)(2,1)} %bitcast.17, bf16[1024,256]{1,0:T(8,128)(2,1)} %copy-done.16, bf16[1024,256]{1,0:T(8,128)(2,1)} %copy-done.15, ...), custom_call_target="tpu_custom_call" | custom-call | flops 6442450944 | bytes 8388608 | tf_op jit(solution)/shard_map/pallas_call | solution.py:222
  64.1 49.4 %all_to_all.21.in_ref = bf16[4,1024,256]{2,1,0:T(8,128)(2,1)S(1)} all-to-all(bf16[4,1024,256]{2,1,0:T(8,128)(2,1)} %bitcast.13), channel_id=1, replica_groups=mesh['y'=4,'z'=8,'mp'=8] {'y'}, dimensions={0} | all-to-all | bytes 4194304 | tf_op jit(solution)/shard_map/all_to_all | solution.py:266
  113.5 5.0 %all-to-all-start.1 = ((f32[8,8,128]{2,1,0:T(8,128)}), f32[8,8,128]{2,1,0:T(8,128)S(1)}, u32[]{:S(2)}, u32[]{:S(2)}) async-start(f32[8,8,128]{2,1,0:T(8,128)} %get-tuple-element.26), calls=%async_computation.1 | async-start | bytes 65536 | tf_op jit(solution)/shard_map/all_to_all | solution.py:265
  118.5 1.1 shard_map.105
  119.5 2.9 %all-to-all-done.1.feat_ref = f32[8,8,128]{2,1,0:T(8,128)S(1)} async-done(((f32[8,8,128]{2,1,0:T(8,128)}), f32[8,8,128]{2,1,0:T(8,128)S(1)}, u32[]{:S(2)}, u32[]{:S(2)}) %all-to-all-start.1) | async-done | bytes 32800 | tf_op jit(solution)/shard_map/all_to_all | solution.py:265
  122.5 8.4 %all-to-all-start.3 = ((bf16[8,128,256]{2,1,0:T(8,128)(2,1)}), bf16[8,128,256]{2,1,0:T(8,128)(2,1)S(1)}, u32[]{:S(2)}, u32[]{:S(2)}) async-start(bf16[8,128,256]{2,1,0:T(8,128)(2,1)} %bitcast.6), calls=%async_computation.3 | async-start | bytes 1048576 | tf_op jit(solution)/shard_map/all_to_all | solution.py:271
  130.9 2.1 %shard_map.104 = (bf16[512,1024]{1,0:T(8,128)(2,1)}, bf16[512,1024]{1,0:T(8,128)(2,1)}) custom-call(s32[1,128]{1,0:T(1,128)S(1)} %bitcast.10, f32[128,128]{1,0:T(8,128)S(1)} %get-tuple-element.18.router_ref, bf16[128,1024]{1,0:T(8,128)(2,1)S(1)} %copy-done.11, bf16[128,1024]{1,0:T(8,128)(2,1)S(1)} %copy-done.12), custom_call_target="tpu_custom_call" | custom-call | flops 268435456 | bytes 3145728 | tf_op jit(solution)/shard_map/pallas_call | solution.py:222
  133.0 15.3 %all-to-all-done.3.part_ref = bf16[8,128,256]{2,1,0:T(8,128)(2,1)S(1)} async-done(((bf16[8,128,256]{2,1,0:T(8,128)(2,1)}), bf16[8,128,256]{2,1,0:T(8,128)(2,1)S(1)}, u32[]{:S(2)}, u32[]{:S(2)}) %all-to-all-start.3) | async-done | bytes 524320 | tf_op jit(solution)/shard_map/all_to_all | solution.py:271
  148.3 1.0 shard_map.106
  (29 shorter events, 2.2 us)
Async XLA Ops:
  0.6 33.2 %copy-start = (bf16[512,1024]{1,0:T(8,128)(2,1)S(1)}, bf16[512,1024]{1,0:T(8,128)(2,1)}, u32[]{:S(2)}) copy-start(bf16[512,1024]{1,0:T(8,128)(2,1)} %query_ref.1) | copy-start | bytes 3145732
  0.6 1.0 copy-start.2
  1.6 0.9 copy-start.3
  2.5 0.7 copy-start.4
  29.2 27.5 %copy-start.13 = (bf16[8,128,256]{2,1,0:T(8,128)(2,1)}, bf16[8,128,256]{2,1,0:T(8,128)(2,1)S(1)}, u32[]{:S(2)}) copy-start(bf16[8,128,256]{2,1,0:T(8,128)(2,1)S(1)} %all_to_all.20) | copy-start | bytes 1572868
  29.2 23.8 %collective-permute-start.2 = (bf16[1024,256]{1,0:T(8,128)(2,1)S(1)}, bf16[1024,256]{1,0:T(8,128)(2,1)S(1)}, u32[]{:S(2)}, u32[]{:S(2)}) collective-permute-start(bf16[1024,256]{1,0:T(8,128)(2,1)S(1)} %bitcast.14), channel_id=1, source_target_pairs={{0,192},{64,0},{128,64},{192,128},{1,193},{65,1},{129,65},{193,129... | collective-permute-start | bytes 1572872 | tf_op jit(solution)/shard_map/ppermute | solution.py:248
  32.3 20.8 %collective-permute-start.1 = (bf16[1024,256]{1,0:T(8,128)(2,1)S(1)}, bf16[1024,256]{1,0:T(8,128)(2,1)S(1)}, u32[]{:S(2)}, u32[]{:S(2)}) collective-permute-start(bf16[1024,256]{1,0:T(8,128)(2,1)S(1)} %bitcast.15), channel_id=1, source_target_pairs={{0,128},{64,192},{128,0},{192,64},{1,129},{65,193},{129,1},{193,65... | collective-permute-start | bytes 1572872 | tf_op jit(solution)/shard_map/ppermute | solution.py:248
  32.9 23.8 %collective-permute-start = (bf16[1024,256]{1,0:T(8,128)(2,1)S(1)}, bf16[1024,256]{1,0:T(8,128)(2,1)S(1)}, u32[]{:S(2)}, u32[]{:S(2)}) collective-permute-start(bf16[1024,256]{1,0:T(8,128)(2,1)S(1)} %bitcast.16), channel_id=1, source_target_pairs={{0,64},{64,128},{128,192},{192,0},{1,65},{65,129},{129,193},{193,1... | collective-permute-start | bytes 1572872 | tf_op jit(solution)/shard_map/ppermute | solution.py:248
  33.9 1.2 copy-start.1
  35.1 0.7 copy-start.5
  35.7 0.7 copy-start.7
  37.2 0.7 copy-start.8
  37.9 0.7 copy-start.9
  38.6 0.7 copy-start.10
  53.0 3.7 %copy-start.14 = (bf16[1024,256]{1,0:T(8,128)(2,1)}, bf16[1024,256]{1,0:T(8,128)(2,1)S(1)}, u32[]{:S(2)}) copy-start(bf16[1024,256]{1,0:T(8,128)(2,1)S(1)} %collective-permute-done.2.kv3) | copy-start | bytes 1572868
  53.0 3.7 %copy-start.15 = (bf16[1024,256]{1,0:T(8,128)(2,1)}, bf16[1024,256]{1,0:T(8,128)(2,1)S(1)}, u32[]{:S(2)}) copy-start(bf16[1024,256]{1,0:T(8,128)(2,1)S(1)} %collective-permute-done.1.kv2) | copy-start | bytes 1572868
  56.7 0.8 copy-start.16
  113.5 17.3 %copy-start.6 = (s32[128]{0:T(128)S(1)}, s32[128]{0:T(128)}, u32[]{:S(2)}) copy-start(s32[128]{0:T(128)} %param.11) | copy-start | bytes 1540
  113.5 17.3 %copy-start.11 = (bf16[128,1024]{1,0:T(8,128)(2,1)S(1)}, bf16[128,1024]{1,0:T(8,128)(2,1)}, u32[]{:S(2)}) copy-start(bf16[128,1024]{1,0:T(8,128)(2,1)} %get-tuple-element.22.att_ref) | copy-start | bytes 786436
  113.5 17.3 %copy-start.12 = (bf16[128,1024]{1,0:T(8,128)(2,1)S(1)}, bf16[128,1024]{1,0:T(8,128)(2,1)}, u32[]{:S(2)}) copy-start(bf16[128,1024]{1,0:T(8,128)(2,1)} %get-tuple-element.23.dq_ref) | copy-start | bytes 786436
  113.5 8.9 %all-to-all-start.1 = ((f32[8,8,128]{2,1,0:T(8,128)}), f32[8,8,128]{2,1,0:T(8,128)S(1)}, u32[]{:S(2)}, u32[]{:S(2)}) async-start(f32[8,8,128]{2,1,0:T(8,128)} %get-tuple-element.26), calls=%async_computation.1 | async-start | bytes 65536 | tf_op jit(solution)/shard_map/all_to_all | solution.py:265
  122.5 25.8 %all-to-all-start.3 = ((bf16[8,128,256]{2,1,0:T(8,128)(2,1)}), bf16[8,128,256]{2,1,0:T(8,128)(2,1)S(1)}, u32[]{:S(2)}, u32[]{:S(2)}) async-start(bf16[8,128,256]{2,1,0:T(8,128)(2,1)} %bitcast.6), calls=%async_computation.3 | async-start | bytes 1048576 | tf_op jit(solution)/shard_map/all_to_all | solution.py:271

commit v2 on v1

--- a/solution.py
+++ b/solution.py
@@ -16,6 +16,9 @@
 LANES = HEADS * HEAD_DIM
 KEYS = ROWS_Y * ROWS_Z * SLOTS
 TILE = 256
+GROUP = 16
+SHARDS = ROWS_Y * ROWS_Z
+PACKED = 2560
 QCHUNK = 256
 FLAG = 64.0
 NEG = -1e30
@@ -79,26 +82,39 @@
 
 
 def attention_kernel(pos_ref, kv0, kv1, kv2, kv3, q_ref, g_ref, c_ref,
-                     att_ref, dq_ref, dkv_ref, feat_ref,
-                     kvs, s_ref, w_ref, at_ref, dqt_ref, top_ref, sum_ref, cen_ref, sem):
+                     att_ref, dq_ref, part0, part1, part2, part3, feat_ref,
+                     lines, kvs, dkv_ref, s_ref, w_ref, at_ref, dqt_ref, top_ref, sum_ref, cen_ref, base_ref, sem):
     row = pos_ref[0]
-    col = pos_ref[1]
+    own = row * ROWS_Z + pos_ref[1]
     block = ROWS_Z * SLOTS
     copies = []
     for k, src in enumerate((kv0, kv1, kv2, kv3)):
         owner = lax.rem(row - k + ROWS_Y, ROWS_Y)
         start = pl.multiple_of(owner * block, block)
-        copies.append(pltpu.make_async_copy(src, kvs.at[pl.ds(start, block), :], sem.at[k]))
+        copies.append(pltpu.make_async_copy(src, lines.at[pl.ds(start, block), :], sem.at[k]))
     for c in copies:
         c.start()
     at_ref[...] = jnp.zeros_like(at_ref)
     dqt_ref[...] = jnp.zeros_like(dqt_ref)
     top_ref[...] = jnp.full_like(top_ref, NEG)
     sum_ref[...] = jnp.zeros_like(sum_ref)
-    tiles = row * (block // TILE) + col * SLOTS // TILE + 1
-    query_id = (row * ROWS_Z + col) * SLOTS
     for c in copies:
         c.wait()
+
+    counts = []
+    for s in range(SHARDS):
+        flags = jnp.where(lines[s * SLOTS : (s + 1) * SLOTS, :HEAD_DIM].astype(F32) < 0.5 * FLAG, 1.0, 0.0)
+        counts.append(jnp.max(jnp.sum(flags, axis=0, keepdims=True)).astype(jnp.int32))
+    base = jnp.int32(0)
+    for s in range(SHARDS):
+        base_ref[s] = base
+        at = pl.multiple_of(base, GROUP)
+        kvs[pl.ds(at, SLOTS), :] = lines[s * SLOTS : (s + 1) * SLOTS, :]
+        base = base + (counts[s] + (GROUP - 1)) // GROUP * GROUP
+    base_ref[SHARDS] = base
+    kvs[pl.ds(pl.multiple_of(base, GROUP), TILE), :] = jnp.zeros((TILE, 2 * HEAD_DIM), BF)
+    query_id = base_ref[own]
+    tiles = (base_ref[own + 1] + (TILE - 1)) // TILE
 
     def scores(t, carry):
         keys = kvs[pl.ds(pl.multiple_of(t * TILE, TILE), TILE), :HEAD_DIM]
@@ -175,11 +191,13 @@
 
     lax.fori_loop(0, tiles, backward, 0)
 
-    def clear(t, carry):
-        dkv_ref[pl.ds(pl.multiple_of(t * TILE, TILE), TILE), :] = jnp.zeros((TILE, 2 * HEAD_DIM), BF)
-        return carry
-
-    lax.fori_loop(tiles, KEYS // TILE, clear, 0)
+    dkv_ref[pl.ds(pl.multiple_of(tiles * TILE, TILE), TILE), :] = jnp.zeros((TILE, 2 * HEAD_DIM), BF)
+    for k, out in enumerate((part0, part1, part2, part3)):
+        first = lax.rem(row + k, ROWS_Y) * ROWS_Z
+        for z in range(ROWS_Z):
+            at = pl.multiple_of(base_ref[first + z], GROUP)
+            rows = dkv_ref[pl.ds(at, SLOTS), :]
+            out[z * SLOTS : (z + 1) * SLOTS, :] = jnp.where(first + z <= own, rows, jnp.zeros_like(rows))
     for h in range(HEADS):
         lanes = slice(h * HEAD_DIM, (h + 1) * HEAD_DIM)
         dq_ref[:, lanes] = jnp.transpose(dqt_ref[:, lanes].astype(BF))
@@ -195,11 +213,13 @@
         qgrad_ref[:, lanes] = dot(place, dq_ref[:, lanes]).astype(BF)
 
 
-def add_rows_kernel(in_ref, out_ref):
-    total = in_ref[0].astype(F32)
-    for k in range(1, ROWS_Y):
-        total += in_ref[k].astype(F32)
-    out_ref[...] = total.astype(BF)
+def add_rows_kernel(in0, in1, in2, in3, out_ref):
+    total = in0[...].astype(F32)
+    for ref in (in1, in2, in3):
+        total += ref[...].astype(F32)
+    total = total.astype(BF)
+    for z in range(ROWS_Z):
+        out_ref[z] = total[z * SLOTS : (z + 1) * SLOTS, :]
 
 
 def place_kv_kernel(sel_ref, router_ref, feat_ref, part_ref, kgrad_ref, vgrad_ref, rgrad_ref):
@@ -250,25 +270,28 @@
     pos = jnp.stack([row, col]).astype(jnp.int32)
     specs = [pl.BlockSpec(memory_space=pltpu.SMEM)] + [pl.BlockSpec(memory_space=pl.ANY)] * 4
     specs += [pl.BlockSpec(memory_space=VMEM)] * 3
-    att, dq, dkv, feat = call(
+    block = ROWS_Z * SLOTS
+    att, dq, *parts, feat = call(
         attention_kernel,
-        [((SLOTS, LANES), BF), ((SLOTS, LANES), BF), ((KEYS, 2 * HEAD_DIM), BF), ((8, 8, SLOTS), F32)],
+        [((SLOTS, LANES), BF)] * 2 + [((block, 2 * HEAD_DIM), BF)] * 4 + [((8, 8, SLOTS), F32)],
         (pos, *lines, q, g, c),
         scratch=[
-            VMEM((KEYS, 2 * HEAD_DIM), BF), VMEM((KEYS, LANES), F32), VMEM((KEYS, LANES), BF),
+            VMEM((KEYS, 2 * HEAD_DIM), BF), VMEM((PACKED + TILE, 2 * HEAD_DIM), BF),
+            VMEM((PACKED + TILE, 2 * HEAD_DIM), BF), VMEM((PACKED, LANES), F32), VMEM((PACKED, LANES), BF),
             VMEM((HEAD_DIM, LANES), F32), VMEM((HEAD_DIM, LANES), F32),
             VMEM((8, LANES), F32), VMEM((8, LANES), F32), VMEM((8, LANES), F32),
+            pltpu.SMEM((SHARDS + 1,), jnp.int32),
             pltpu.SemaphoreType.DMA((4,)),
         ],
         specs=specs,
-        cost=(12 * KEYS * LANES * HEAD_DIM, 8 << 20))
+        cost=(12 * PACKED * LANES * HEAD_DIM, 8 << 20))
+    moved = [lax.ppermute(parts[k], "y", [(s, (s + k) % ROWS_Y) for s in range(ROWS_Y)]) for k in range(1, ROWS_Y)]
     feat = lax.all_to_all(feat, "mp", 0, 0, tiled=True)
-    part = lax.all_to_all(dkv.reshape(ROWS_Y, ROWS_Z * SLOTS, 2 * HEAD_DIM), "y", 0, 0, tiled=True)
     mixed, qgrad = call(place_q_kernel, [((TOK, LANES), BF)] * 2, (sel, router, att, dq),
                         cost=(4 * SLOTS * TOK * LANES, 3 << 20))
-    (part,) = call(add_rows_kernel, [((ROWS_Z * SLOTS, 2 * HEAD_DIM), BF)], (part,),
+    (part,) = call(add_rows_kernel, [((ROWS_Z, SLOTS, 2 * HEAD_DIM), BF)], (parts[0], *moved),
                    cost=(1 << 20, 3 << 20))
-    part = lax.all_to_all(part.reshape(ROWS_Z, SLOTS, 2 * HEAD_DIM), "z", 0, 0, tiled=True)
+    part = lax.all_to_all(part, "z", 0, 0, tiled=True)
     kgrad, vgrad, rgrad = call(
         place_kv_kernel,
         [((TOK, HEAD_DIM), BF)] * 2 + [((1, TOK), F32)],

time: 152 us -> 127 us (0.84); the launches traced: 149 us -> 126 us
  blocking collectives: 75.2 us -> 25.8 us
  waiting for transfers between devices: 35.1 us -> 49 us
  starting transfers between devices: 17.9 us -> 29.5 us
    all_to_all x1 -> x0, blocking collectives: 49.4 us -> none  [shards(): lax.all_to_all(dkv.reshape(ROWS_Y, ROWS_Z * SLOTS, 2 * HEAD_DIM), 'y', 0,...]
    ppermute x0 -> x3, waiting for transfers between devices: none -> 17.4 us  [shards(): lax.ppermute(parts[k], 'y', [(s, (s + k) % ROWS_Y) for s in range(ROWS_Y)])]
    ppermute x0 -> x3, starting transfers between devices: none -> 13.3 us  [shards(): lax.ppermute(parts[k], 'y', [(s, (s + k) % ROWS_Y) for s in range(ROWS_Y)])]
    all_to_all x1, waiting for transfers between devices: 2.92 us -> 0.01 us  [shards(): feat = lax.all_to_all(feat, 'mp', 0, 0, tiled=True)]
    all_to_all x1, starting transfers between devices: 8.38 us -> 6.72 us  [shards(): part = lax.all_to_all(part, 'z', 0, 0, tiled=True)]
  transfers between devices with their start and end apart: 5 -> 8, of which waited for: 4 -> 5; matrix products, arithmetic and copies ran while one was open for 0% -> 0% of each run, Pallas kernels for 3% -> 3%
where the time goes in v2:
time: 127 us; the launch traced here: 126 us
  waiting for transfers between devices  49 us (39%)
  starting transfers between devices  29.5 us (23%)
  blocking collectives  25.8 us (20%)
  Pallas kernels  12.2 us (10%)
  local copies, waits for them, and re-layouts  8.41 us (7%)
    all_to_all x1, blocking collectives, shards(): line = lax.all_to_all(own, 'z', 0, 0, tiled=True)  25.8 us
    ppermute x3, waiting for transfers between devices, shards(): lax.ppermute(line, 'y', [(s, (s + k) % ROWS_Y) for s in range(ROWS_Y)])  17.5 us
    ppermute x3, waiting for transfers between devices, shards(): lax.ppermute(parts[k], 'y', [(s, (s + k) % ROWS_Y) for s in range(ROWS_Y)])  17.4 us
    all_to_all x1, waiting for transfers between devices, shards(): part = lax.all_to_all(part, 'z', 0, 0, tiled=True)  14.2 us
    ppermute x3, starting transfers between devices, shards(): lax.ppermute(parts[k], 'y', [(s, (s + k) % ROWS_Y) for s in range(ROWS_Y)])  13.3 us
    pallas_call x6, Pallas kernels, call(): pl.pallas_call(kernel, out_shape=[jax.ShapeDtypeStruct(s, d) for s, d in...  12.2 us
    unnamed x34, local copies, waits for them, and re-layouts  8.41 us
    all_to_all x1, starting transfers between devices, shards(): part = lax.all_to_all(part, 'z', 0, 0, tiled=True)  6.72 us
  transfers between devices with their start and end apart: 8, of which 5 were waited for; matrix products, arithmetic and copies ran while one was open for 0% of the time, Pallas kernels for 3%

profile of v2, /device:TPU:2, one launch (start us, length us, event | category | flops | bytes accessed | tf_op | source)
XLA Modules:
  0.0 126.2 jit_solution(10555071190890243921)
XLA Ops:
  0.7 1.0 copy-done.3
  1.6 0.9 copy-done.4
  3.5 25.8 %all_to_all.15 = bf16[8,128,256]{2,1,0:T(8,128)(2,1)S(1)} all-to-all(bf16[8,128,256]{2,1,0:T(8,128)(2,1)S(1)} %shard_map.102), channel_id=1, replica_groups=mesh['y'=4,'z'=8,'mp'=8] {'z'}, dimensions={0} | all-to-all | bytes 1048576 | tf_op jit(solution)/shard_map/all_to_all | solution.py:260
  29.2 3.0 %collective-permute-start.2 = (bf16[1024,256]{1,0:T(8,128)(2,1)S(1)}, bf16[1024,256]{1,0:T(8,128)(2,1)S(1)}, u32[]{:S(2)}, u32[]{:S(2)}) collective-permute-start(bf16[1024,256]{1,0:T(8,128)(2,1)S(1)} %bitcast.11), channel_id=1, source_target_pairs={{0,192},{64,0},{128,64},{192,128},{1,193},{65,1},{129,65},{193,129... | collective-permute-start | bytes 1572872 | tf_op jit(solution)/shard_map/ppermute | solution.py:268
  32.9 1.0 collective-permute-start
  34.5 1.2 copy-done.1
  35.8 0.8 shard_map.101
  37.3 0.7 copy-done.9
  38.0 0.7 copy-done.10
  39.3 13.8 %collective-permute-done.2.kv3 = bf16[1024,256]{1,0:T(8,128)(2,1)S(1)} collective-permute-done((bf16[1024,256]{1,0:T(8,128)(2,1)S(1)}, bf16[1024,256]{1,0:T(8,128)(2,1)S(1)}, u32[]{:S(2)}, u32[]{:S(2)}) %collective-permute-start.2) | collective-permute-done | bytes 524320 | tf_op jit(solution)/shard_map/ppermute | solution.py:268
  53.0 3.7 %collective-permute-done.kv1 = bf16[1024,256]{1,0:T(8,128)(2,1)S(1)} collective-permute-done((bf16[1024,256]{1,0:T(8,128)(2,1)S(1)}, bf16[1024,256]{1,0:T(8,128)(2,1)S(1)}, u32[]{:S(2)}, u32[]{:S(2)}) %collective-permute-start) | collective-permute-done | bytes 524320 | tf_op jit(solution)/shard_map/ppermute | solution.py:268
  56.7 0.8 copy-done.16
  57.5 7.0 %shard_map.103 = (bf16[128,1024]{1,0:T(8,128)(2,1)}, bf16[128,1024]{1,0:T(8,128)(2,1)}, bf16[1024,256]{1,0:T(8,128)(2,1)}, bf16[1024,256]{1,0:T(8,128)(2,1)}, bf...) custom-call(s32[2]{0:T(128)} %pad_add_fusion.pos_ref, bf16[1024,256]{1,0:T(8,128)(2,1)} %bitcast.14, ...), custom_call_target="tpu_custom_call" | custom-call | flops 4026531840 | bytes 8388608 | tf_op jit(solution)/shard_map/pallas_call | solution.py:242
  64.6 3.0 %collective-permute-start.3 = (bf16[1024,256]{1,0:T(8,128)(2,1)}, bf16[1024,256]{1,0:T(8,128)(2,1)S(1)}, u32[]{:S(2)}, u32[]{:S(2)}) collective-permute-start(bf16[1024,256]{1,0:T(8,128)(2,1)} %get-tuple-element.31), channel_id=1, source_target_pairs={{0,64},{64,128},{128,192},{192,0},{1,65},{65,129},{129,193},{193,1... | collective-permute-start | bytes 1572872 | tf_op jit(solution)/shard_map/ppermute | solution.py:288
  67.5 10.4 %collective-permute-start.4 = (bf16[1024,256]{1,0:T(8,128)(2,1)}, bf16[1024,256]{1,0:T(8,128)(2,1)S(1)}, u32[]{:S(2)}, u32[]{:S(2)}) collective-permute-start(bf16[1024,256]{1,0:T(8,128)(2,1)} %get-tuple-element.32), channel_id=1, source_target_pairs={{0,128},{64,192},{128,0},{192,64},{1,129},{65,193},{129,1},{193,65... | collective-permute-start | bytes 1572872 | tf_op jit(solution)/shard_map/ppermute | solution.py:288
  77.9 4.8 %all-to-all-start.1 = ((f32[8,8,128]{2,1,0:T(8,128)}), f32[8,8,128]{2,1,0:T(8,128)S(1)}, u32[]{:S(2)}, u32[]{:S(2)}) async-start(f32[8,8,128]{2,1,0:T(8,128)} %get-tuple-element.29), calls=%async_computation.1 | async-start | bytes 65536 | tf_op jit(solution)/shard_map/all_to_all | solution.py:289
  82.7 5.8 %collective-permute-done.3.in1 = bf16[1024,256]{1,0:T(8,128)(2,1)S(1)} collective-permute-done((bf16[1024,256]{1,0:T(8,128)(2,1)}, bf16[1024,256]{1,0:T(8,128)(2,1)S(1)}, u32[]{:S(2)}, u32[]{:S(2)}) %collective-permute-start.3) | collective-permute-done | bytes 524320 | tf_op jit(solution)/shard_map/ppermute | solution.py:288
  88.5 11.6 %collective-permute-done.4.in2 = bf16[1024,256]{1,0:T(8,128)(2,1)S(1)} collective-permute-done((bf16[1024,256]{1,0:T(8,128)(2,1)}, bf16[1024,256]{1,0:T(8,128)(2,1)S(1)}, u32[]{:S(2)}, u32[]{:S(2)}) %collective-permute-start.4) | collective-permute-done | bytes 524320 | tf_op jit(solution)/shard_map/ppermute | solution.py:288
  100.1 1.0 copy-done.2
  101.2 1.1 shard_map.105
  102.2 6.7 %all-to-all-start.2 = ((bf16[8,128,256]{2,1,0:T(8,128)(2,1)}), bf16[8,128,256]{2,1,0:T(8,128)(2,1)S(1)}, u32[]{:S(2)}, u32[]{:S(2)}) async-start(bf16[8,128,256]{2,1,0:T(8,128)(2,1)} %shard_map.105), calls=%async_computation.2 | async-start | bytes 1048576 | tf_op jit(solution)/shard_map/all_to_all | solution.py:294
  109.0 2.1 %shard_map.104 = (bf16[512,1024]{1,0:T(8,128)(2,1)}, bf16[512,1024]{1,0:T(8,128)(2,1)}) custom-call(s32[1,128]{1,0:T(1,128)S(1)} %bitcast.8, f32[128,128]{1,0:T(8,128)S(1)} %get-tuple-element.21.router_ref, bf16[128,1024]{1,0:T(8,128)(2,1)S(1)} %copy-done.11, bf16[128,1024]{1,0:T(8,128)(2,1)S(1)} %copy-done.12), custom_call_target="tpu_custom_call" | custom-call | flops 268435456 | bytes 3145728 | tf_op jit(solution)/shard_map/pallas_call | solution.py:242
  111.1 14.2 %all-to-all-done.2.part_ref = bf16[8,128,256]{2,1,0:T(8,128)(2,1)S(1)} async-done(((bf16[8,128,256]{2,1,0:T(8,128)(2,1)}), bf16[8,128,256]{2,1,0:T(8,128)(2,1)S(1)}, u32[]{:S(2)}, u32[]{:S(2)}) %all-to-all-start.2) | async-done | bytes 524320 | tf_op jit(solution)/shard_map/all_to_all | solution.py:294
  125.2 1.0 shard_map.106
  (34 shorter events, 3.6 us)
Async XLA Ops:
  0.6 33.2 %copy-start = (bf16[512,1024]{1,0:T(8,128)(2,1)S(1)}, bf16[512,1024]{1,0:T(8,128)(2,1)}, u32[]{:S(2)}) copy-start(bf16[512,1024]{1,0:T(8,128)(2,1)} %query_ref.1) | copy-start | bytes 3145732
  0.6 1.0 copy-start.3
  1.6 0.9 copy-start.4
  29.2 7.3 %copy-start.13 = (bf16[8,128,256]{2,1,0:T(8,128)(2,1)}, bf16[8,128,256]{2,1,0:T(8,128)(2,1)S(1)}, u32[]{:S(2)}) copy-start(bf16[8,128,256]{2,1,0:T(8,128)(2,1)S(1)} %all_to_all.15) | copy-start | bytes 1572868
  29.2 23.8 %collective-permute-start.2 = (bf16[1024,256]{1,0:T(8,128)(2,1)S(1)}, bf16[1024,256]{1,0:T(8,128)(2,1)S(1)}, u32[]{:S(2)}, u32[]{:S(2)}) collective-permute-start(bf16[1024,256]{1,0:T(8,128)(2,1)S(1)} %bitcast.11), channel_id=1, source_target_pairs={{0,192},{64,0},{128,64},{192,128},{1,193},{65,1},{129,65},{193,129... | collective-permute-start | bytes 1572872 | tf_op jit(solution)/shard_map/ppermute | solution.py:268
  32.3 20.8 %collective-permute-start.1 = (bf16[1024,256]{1,0:T(8,128)(2,1)S(1)}, bf16[1024,256]{1,0:T(8,128)(2,1)S(1)}, u32[]{:S(2)}, u32[]{:S(2)}) collective-permute-start(bf16[1024,256]{1,0:T(8,128)(2,1)S(1)} %bitcast.12), channel_id=1, source_target_pairs={{0,128},{64,192},{128,0},{192,64},{1,129},{65,193},{129,1},{193,65... | collective-permute-start | bytes 1572872 | tf_op jit(solution)/shard_map/ppermute | solution.py:268
  32.9 23.8 %collective-permute-start = (bf16[1024,256]{1,0:T(8,128)(2,1)S(1)}, bf16[1024,256]{1,0:T(8,128)(2,1)S(1)}, u32[]{:S(2)}, u32[]{:S(2)}) collective-permute-start(bf16[1024,256]{1,0:T(8,128)(2,1)S(1)} %bitcast.13), channel_id=1, source_target_pairs={{0,64},{64,128},{128,192},{192,0},{1,65},{65,129},{129,193},{193,1... | collective-permute-start | bytes 1572872 | tf_op jit(solution)/shard_map/ppermute | solution.py:268
  33.9 0.7 copy-start.7
  33.9 0.7 copy-start.6
  34.5 1.2 copy-start.1
  36.6 0.7 copy-start.8
  37.3 0.7 copy-start.9
  38.0 0.7 copy-start.10
  53.0 3.7 %copy-start.14 = (bf16[1024,256]{1,0:T(8,128)(2,1)}, bf16[1024,256]{1,0:T(8,128)(2,1)S(1)}, u32[]{:S(2)}) copy-start(bf16[1024,256]{1,0:T(8,128)(2,1)S(1)} %collective-permute-done.2.kv3) | copy-start | bytes 1572868
  53.0 3.7 %copy-start.15 = (bf16[1024,256]{1,0:T(8,128)(2,1)}, bf16[1024,256]{1,0:T(8,128)(2,1)S(1)}, u32[]{:S(2)}) copy-start(bf16[1024,256]{1,0:T(8,128)(2,1)S(1)} %collective-permute-done.1.kv2) | copy-start | bytes 1572868
  56.7 0.8 copy-start.16
  64.6 24.0 %collective-permute-start.3 = (bf16[1024,256]{1,0:T(8,128)(2,1)}, bf16[1024,256]{1,0:T(8,128)(2,1)S(1)}, u32[]{:S(2)}, u32[]{:S(2)}) collective-permute-start(bf16[1024,256]{1,0:T(8,128)(2,1)} %get-tuple-element.31), channel_id=1, source_target_pairs={{0,64},{64,128},{128,192},{192,0},{1,65},{65,129},{129,193},{193,1... | collective-permute-start | bytes 1572872 | tf_op jit(solution)/shard_map/ppermute | solution.py:288
  67.5 32.6 %collective-permute-start.4 = (bf16[1024,256]{1,0:T(8,128)(2,1)}, bf16[1024,256]{1,0:T(8,128)(2,1)S(1)}, u32[]{:S(2)}, u32[]{:S(2)}) collective-permute-start(bf16[1024,256]{1,0:T(8,128)(2,1)} %get-tuple-element.32), channel_id=1, source_target_pairs={{0,128},{64,192},{128,0},{192,64},{1,129},{65,193},{129,1},{193,65... | collective-permute-start | bytes 1572872 | tf_op jit(solution)/shard_map/ppermute | solution.py:288
  77.9 22.2 %collective-permute-start.5 = (bf16[1024,256]{1,0:T(8,128)(2,1)}, bf16[1024,256]{1,0:T(8,128)(2,1)S(1)}, u32[]{:S(2)}, u32[]{:S(2)}) collective-permute-start(bf16[1024,256]{1,0:T(8,128)(2,1)} %get-tuple-element.33), channel_id=1, source_target_pairs={{0,192},{64,0},{128,64},{192,128},{1,193},{65,1},{129,65},{193,129... | collective-permute-start | bytes 1572872 | tf_op jit(solution)/shard_map/ppermute | solution.py:288
  77.9 24.3 %all-to-all-start.1 = ((f32[8,8,128]{2,1,0:T(8,128)}), f32[8,8,128]{2,1,0:T(8,128)S(1)}, u32[]{:S(2)}, u32[]{:S(2)}) async-start(f32[8,8,128]{2,1,0:T(8,128)} %get-tuple-element.29), calls=%async_computation.1 | async-start | bytes 65536 | tf_op jit(solution)/shard_map/all_to_all | solution.py:289
  100.1 1.0 copy-start.2
  102.2 6.7 %copy-start.11 = (bf16[128,1024]{1,0:T(8,128)(2,1)S(1)}, bf16[128,1024]{1,0:T(8,128)(2,1)}, u32[]{:S(2)}) copy-start(bf16[128,1024]{1,0:T(8,128)(2,1)} %get-tuple-element.25.att_ref) | copy-start | bytes 786436
  102.2 6.7 %copy-start.12 = (bf16[128,1024]{1,0:T(8,128)(2,1)S(1)}, bf16[128,1024]{1,0:T(8,128)(2,1)}, u32[]{:S(2)}) copy-start(bf16[128,1024]{1,0:T(8,128)(2,1)} %get-tuple-element.26.dq_ref) | copy-start | bytes 786436
  102.2 23.0 %all-to-all-start.2 = ((bf16[8,128,256]{2,1,0:T(8,128)(2,1)}), bf16[8,128,256]{2,1,0:T(8,128)(2,1)S(1)}, u32[]{:S(2)}, u32[]{:S(2)}) async-start(bf16[8,128,256]{2,1,0:T(8,128)(2,1)} %shard_map.105), calls=%async_computation.2 | async-start | bytes 1048576 | tf_op jit(solution)/shard_map/all_to_all | solution.py:294
  (1 other events, 0.7 us)

commit v3 on v2

--- a/solution.py
+++ b/solution.py
@@ -14,8 +14,7 @@
 ROWS_Y = 4
 ROWS_Z = 8
 LANES = HEADS * HEAD_DIM
-KEYS = ROWS_Y * ROWS_Z * SLOTS
-TILE = 256
+TILE = 512
 GROUP = 16
 SHARDS = ROWS_Y * ROWS_Z
 PACKED = 2560
@@ -29,7 +28,7 @@
 NT = (((1,), (1,)), ((), ()))
 NN = (((1,), (0,)), ((), ()))
 VMEM = pltpu.VMEM
-LIMIT = 60 * 1024 * 1024
+LIMIT = 34 * 1024 * 1024
 
 
 def dot(a, b, dims=NN):
@@ -55,11 +54,20 @@
     return jnp.where(mask, 1.0, 0.0).astype(BF)
 
 
-def select_kv_kernel(sel_ref, key_ref, value_ref, out_ref):
+def select_kv_kernel(sel_hbm, key_hbm, value_hbm, out_ref, sel_ref, key_ref, value_ref, sem):
+    copies = [
+        pltpu.make_async_copy(src, dst, sem.at[i])
+        for i, (src, dst) in enumerate(((sel_hbm, sel_ref), (key_hbm, key_ref), (value_hbm, value_ref)))
+    ]
+    for c in copies:
+        c.start()
+    copies[0].wait()
     sel = sel_ref[...]
     pick = one_hot(picker(sel))
     live = column_of(sel.astype(F32)) >= 0.0
+    copies[1].wait()
     key = jnp.where(live, dot(pick, key_ref[...]), FLAG).astype(BF)
+    copies[2].wait()
     value = dot(pick, value_ref[...]).astype(BF)
     for copy in range(ROWS_Z):
         out_ref[copy, :, :HEAD_DIM] = key
@@ -83,41 +91,38 @@
 
 def attention_kernel(pos_ref, kv0, kv1, kv2, kv3, q_ref, g_ref, c_ref,
                      att_ref, dq_ref, part0, part1, part2, part3, feat_ref,
-                     lines, kvs, dkv_ref, s_ref, w_ref, at_ref, dqt_ref, top_ref, sum_ref, cen_ref, base_ref, sem):
+                     kvs, dkv_ref, s_ref, w_ref, at_ref, dqt_ref, top_ref, sum_ref, cen_ref, tops_ref, base_ref):
     row = pos_ref[0]
-    own = row * ROWS_Z + pos_ref[1]
-    block = ROWS_Z * SLOTS
-    copies = []
-    for k, src in enumerate((kv0, kv1, kv2, kv3)):
-        owner = lax.rem(row - k + ROWS_Y, ROWS_Y)
-        start = pl.multiple_of(owner * block, block)
-        copies.append(pltpu.make_async_copy(src, lines.at[pl.ds(start, block), :], sem.at[k]))
-    for c in copies:
-        c.start()
+    col = pos_ref[1]
+    own = row * ROWS_Z + col
     at_ref[...] = jnp.zeros_like(at_ref)
     dqt_ref[...] = jnp.zeros_like(dqt_ref)
     top_ref[...] = jnp.full_like(top_ref, NEG)
     sum_ref[...] = jnp.zeros_like(sum_ref)
-    for c in copies:
-        c.wait()
-
-    counts = []
-    for s in range(SHARDS):
-        flags = jnp.where(lines[s * SLOTS : (s + 1) * SLOTS, :HEAD_DIM].astype(F32) < 0.5 * FLAG, 1.0, 0.0)
-        counts.append(jnp.max(jnp.sum(flags, axis=0, keepdims=True)).astype(jnp.int32))
+
+    lines = (kv0, kv1, kv2, kv3)
+    counts = {}
+    for k in reversed(range(ROWS_Y)):
+        for z in range(ROWS_Z):
+            flags = lines[k][z * SLOTS : (z + 1) * SLOTS, :HEAD_DIM].astype(F32) < 0.5 * FLAG
+            live = jnp.sum(jnp.where(flags, 1.0, 0.0), axis=0, keepdims=True)
+            count = jnp.max(live).astype(jnp.int32)
+            past = z <= col if k == 0 else k <= row
+            counts[k, z] = jnp.where(past, (count + (GROUP - 1)) // GROUP * GROUP, 0)
     base = jnp.int32(0)
-    for s in range(SHARDS):
-        base_ref[s] = base
-        at = pl.multiple_of(base, GROUP)
-        kvs[pl.ds(at, SLOTS), :] = lines[s * SLOTS : (s + 1) * SLOTS, :]
-        base = base + (counts[s] + (GROUP - 1)) // GROUP * GROUP
-    base_ref[SHARDS] = base
+    for k in reversed(range(ROWS_Y)):
+        first = lax.rem(row - k + ROWS_Y, ROWS_Y) * ROWS_Z
+        for z in range(ROWS_Z):
+            base_ref[first + z] = base
+            kvs[pl.ds(pl.multiple_of(base, GROUP), SLOTS), :] = lines[k][z * SLOTS : (z + 1) * SLOTS, :]
+            base = base + counts[k, z]
     kvs[pl.ds(pl.multiple_of(base, GROUP), TILE), :] = jnp.zeros((TILE, 2 * HEAD_DIM), BF)
     query_id = base_ref[own]
-    tiles = (base_ref[own + 1] + (TILE - 1)) // TILE
+    tiles = (base + (TILE - 1)) // TILE
 
     def scores(t, carry):
-        keys = kvs[pl.ds(pl.multiple_of(t * TILE, TILE), TILE), :HEAD_DIM]
+        rows = pl.ds(pl.multiple_of(t * TILE, TILE), TILE)
+        keys = kvs[rows, :HEAD_DIM]
         kid = t * TILE + lax.broadcasted_iota(jnp.int32, (TILE, SLOTS), 0)
         qid = query_id + lax.broadcasted_iota(jnp.int32, (TILE, SLOTS), 1)
         dead = jnp.broadcast_to(keys[:, :1].astype(F32), (TILE, SLOTS)) > 0.5 * FLAG
@@ -126,36 +131,37 @@
         for c in range(LANES // QCHUNK):
             lanes = slice(c * QCHUNK, (c + 1) * QCHUNK)
             s = dot(keys, q_ref[lanes, :], NT) * (SCALE * LOG2E) + bias
-            s_ref[pl.ds(pl.multiple_of(t * TILE, TILE), TILE), lanes] = s
-            part = jnp.max(s.reshape(TILE // 8, 8, QCHUNK), axis=0)
-            top_ref[:, lanes] = jnp.maximum(top_ref[:, lanes], part)
+            s = s.reshape(TILE // 8, 8, QCHUNK)
+            old = top_ref[:, lanes]
+            new = jnp.maximum(old, jnp.max(s, axis=0))
+            e = jnp.exp2(s - new[None])
+            top_ref[:, lanes] = new
+            tops_ref[t, :, lanes] = new
+            sum_ref[:, lanes] = sum_ref[:, lanes] * jnp.exp2(old - new) + jnp.sum(e, axis=0)
+            s_ref[rows, lanes] = e.reshape(TILE, QCHUNK)
         return carry
 
     lax.fori_loop(0, tiles, scores, 0)
-    top_ref[...] = jnp.broadcast_to(jnp.max(top_ref[...], axis=0, keepdims=True), top_ref.shape)
-
-    def exponent(t, carry):
+    top = jnp.max(top_ref[...], axis=0, keepdims=True)
+    total = jnp.sum(sum_ref[...] * jnp.exp2(top_ref[...] - top), axis=0, keepdims=True)
+    top_ref[...] = jnp.broadcast_to(top, top_ref.shape)
+    sum_ref[...] = jnp.broadcast_to(1.0 / total, sum_ref.shape)
+
+    def forward(t, carry):
         rows = pl.ds(pl.multiple_of(t * TILE, TILE), TILE)
+        values = kvs[rows, HEAD_DIM:]
+        value_t = jnp.transpose(values)
+        acc = jnp.zeros((TILE, HEAD_DIM), F32)
         for c in range(LANES // QCHUNK):
             lanes = slice(c * QCHUNK, (c + 1) * QCHUNK)
-            e = jnp.exp2(s_ref[rows, lanes] - top_ref[:1, lanes])
-            s_ref[rows, lanes] = e
-            sum_ref[:, lanes] += jnp.sum(e.reshape(TILE // 8, 8, QCHUNK), axis=0)
-        return carry
-
-    lax.fori_loop(0, tiles, exponent, 0)
-    total = jnp.sum(sum_ref[...], axis=0, keepdims=True)
-    sum_ref[...] = jnp.broadcast_to(1.0 / total, sum_ref.shape)
-
-    def forward(t, carry):
-        rows = pl.ds(pl.multiple_of(t * TILE, TILE), TILE)
-        value_t = jnp.transpose(kvs[rows, HEAD_DIM:])
-        for c in range(LANES // QCHUNK):
-            lanes = slice(c * QCHUNK, (c + 1) * QCHUNK)
-            w = (s_ref[rows, lanes] * sum_ref[:1, lanes]).astype(BF)
+            factor = jnp.exp2(tops_ref[t, :, lanes] - top_ref[:, lanes]) * sum_ref[:, lanes]
+            w = s_ref[rows, lanes].reshape(TILE // 8, 8, QCHUNK) * factor[None]
+            w = w.reshape(TILE, QCHUNK).astype(BF)
             w_ref[rows, lanes] = w
             at_ref[:, lanes] += dot(value_t, w)
-        dkv_ref[rows, HEAD_DIM:] = dot(w_ref[rows, :], g_ref[...]).astype(BF)
+            acc += dot(w, g_ref[lanes, :])
+            s_ref[rows, lanes] = dot(values, g_ref[lanes, :], NT)
+        dkv_ref[rows, HEAD_DIM:] = acc.astype(BF)
         return carry
 
     lax.fori_loop(0, tiles, forward, 0)
@@ -177,13 +183,13 @@
 
     def backward(t, carry):
         rows = pl.ds(pl.multiple_of(t * TILE, TILE), TILE)
-        values = kvs[rows, HEAD_DIM:]
         key_t = jnp.transpose(kvs[rows, :HEAD_DIM])
         acc = jnp.zeros((TILE, HEAD_DIM), F32)
         for c in range(LANES // QCHUNK):
             lanes = slice(c * QCHUNK, (c + 1) * QCHUNK)
-            slope = dot(values, g_ref[lanes, :], NT)
-            ds = (w_ref[rows, lanes].astype(F32) * (slope - cen_ref[:1, lanes]) * SCALE).astype(BF)
+            slope = s_ref[rows, lanes].reshape(TILE // 8, 8, QCHUNK)
+            w = w_ref[rows, lanes].astype(F32).reshape(TILE // 8, 8, QCHUNK)
+            ds = (w * (slope - cen_ref[:, lanes][None]) * SCALE).reshape(TILE, QCHUNK).astype(BF)
             dqt_ref[:, lanes] += dot(key_t, ds)
             acc += dot(ds, q_ref[lanes, :])
         dkv_ref[rows, :HEAD_DIM] = acc.astype(BF)
@@ -238,16 +244,36 @@
     rgrad_ref[...] = jnp.sum(jnp.where(picker(sel_ref[...]), terms, 0.0), axis=0, keepdims=True)
 
 
-def call(kernel, outs, args, scratch=(), specs=None, cost=None):
+def call(kernel, outs, args, scratch=(), specs=None, cost=None, limit=12 * 1024 * 1024):
     return pl.pallas_call(
         kernel,
         out_shape=[jax.ShapeDtypeStruct(s, d) for s, d in outs],
         in_specs=specs or [pl.BlockSpec(memory_space=VMEM)] * len(args),
         out_specs=[pl.BlockSpec(memory_space=VMEM)] * len(outs),
         scratch_shapes=list(scratch),
-        compiler_params=pltpu.CompilerParams(vmem_limit_bytes=LIMIT if scratch else 24 * 1024 * 1024),
+        compiler_params=pltpu.CompilerParams(vmem_limit_bytes=limit),
         cost_estimate=pl.CostEstimate(flops=cost[0], bytes_accessed=cost[1], transcendentals=0),
     )(*args)
+
+
+def attend(pos, kv0, kv1, kv2, kv3, q, g, c):
+    specs = [pl.BlockSpec(memory_space=pltpu.SMEM)] + [pl.BlockSpec(memory_space=VMEM)] * 7
+    block = ROWS_Z * SLOTS
+    return call(
+        attention_kernel,
+        [((SLOTS, LANES), BF)] * 2 + [((block, 2 * HEAD_DIM), BF)] * 4 + [((8, 8, SLOTS), F32)],
+        (pos, kv0, kv1, kv2, kv3, q, g, c),
+        scratch=[
+            VMEM((PACKED + TILE, 2 * HEAD_DIM), BF),
+            VMEM((PACKED + TILE, 2 * HEAD_DIM), BF), VMEM((PACKED, LANES), F32), VMEM((PACKED, LANES), BF),
+            VMEM((HEAD_DIM, LANES), F32), VMEM((HEAD_DIM, LANES), F32),
+            VMEM((8, LANES), F32), VMEM((8, LANES), F32), VMEM((8, LANES), F32),
+            VMEM((PACKED // TILE, 8, LANES), F32),
+            pltpu.SMEM((SHARDS,), jnp.int32),
+        ],
+        specs=specs,
+        cost=(12 * PACKED * LANES * HEAD_DIM, 8 << 20),
+        limit=LIMIT)
 
 
 def shards(query_rows, key_rows, value_rows, cotangent, router_logits, selection):
@@ -256,7 +282,10 @@
     row = lax.axis_index("y")
     col = lax.axis_index("z")
     (own,) = call(select_kv_kernel, [((ROWS_Z, SLOTS, 2 * HEAD_DIM), BF)], (sel, key_rows, value_rows),
-                  cost=(2 * SLOTS * TOK * 256, 1 << 20))
+                  scratch=[VMEM((1, SLOTS), jnp.int32), VMEM((TOK, HEAD_DIM), BF), VMEM((TOK, HEAD_DIM), BF),
+                           pltpu.SemaphoreType.DMA((3,))],
+                  specs=[pl.BlockSpec(memory_space=pltpu.HBM)] * 3,
+                  cost=(2 * SLOTS * TOK * 256, 1 << 20), limit=60 * 1024 * 1024)
     line = lax.all_to_all(own, "z", 0, 0, tiled=True)
     q, g, c, router = call(
         select_q_kernel,
@@ -268,23 +297,7 @@
         lax.ppermute(line, "y", [(s, (s + k) % ROWS_Y) for s in range(ROWS_Y)]) for k in range(1, ROWS_Y)
     ]
     pos = jnp.stack([row, col]).astype(jnp.int32)
-    specs = [pl.BlockSpec(memory_space=pltpu.SMEM)] + [pl.BlockSpec(memory_space=pl.ANY)] * 4
-    specs += [pl.BlockSpec(memory_space=VMEM)] * 3
-    block = ROWS_Z * SLOTS
-    att, dq, *parts, feat = call(
-        attention_kernel,
-        [((SLOTS, LANES), BF)] * 2 + [((block, 2 * HEAD_DIM), BF)] * 4 + [((8, 8, SLOTS), F32)],
-        (pos, *lines, q, g, c),
-        scratch=[
-            VMEM((KEYS, 2 * HEAD_DIM), BF), VMEM((PACKED + TILE, 2 * HEAD_DIM), BF),
-            VMEM((PACKED + TILE, 2 * HEAD_DIM), BF), VMEM((PACKED, LANES), F32), VMEM((PACKED, LANES), BF),
-            VMEM((HEAD_DIM, LANES), F32), VMEM((HEAD_DIM, LANES), F32),
-            VMEM((8, LANES), F32), VMEM((8, LANES), F32), VMEM((8, LANES), F32),
-            pltpu.SMEM((SHARDS + 1,), jnp.int32),
-            pltpu.SemaphoreType.DMA((4,)),
-        ],
-        specs=specs,
-        cost=(12 * PACKED * LANES * HEAD_DIM, 8 << 20))
+    att, dq, *parts, feat = attend(pos, *lines, q, g, c)
     moved = [lax.ppermute(parts[k], "y", [(s, (s + k) % ROWS_Y) for s in range(ROWS_Y)]) for k in range(1, ROWS_Y)]
     feat = lax.all_to_all(feat, "mp", 0, 0, tiled=True)
     mixed, qgrad = call(place_q_kernel, [((TOK, LANES), BF)] * 2, (sel, router, att, dq),

time: 127 us -> 118 us (0.929)
  local copies, waits for them, and re-layouts: 8.41 us -> 2.61 us
  starting transfers between devices: 29.5 us -> 24 us
  waiting for transfers between devices: 49 us -> 51.5 us
    unnamed x34 -> x12, local copies, waits for them, and re-layouts: 8.41 us -> 2.61 us
    ppermute x3, starting transfers between devices: 13.3 us -> 9.2 us  [shards(): lax.ppermute(parts[k], 'y', [(s, (s + k) % ROWS_Y) for s in range(ROWS_Y)])]
    ppermute x3, waiting for transfers between devices: 17.5 us -> 20.1 us  [shards(): lax.ppermute(line, 'y', [(s, (s + k) % ROWS_Y) for s in range(ROWS_Y)])]
    all_to_all x1, starting transfers between devices: 6.72 us -> 5.37 us  [shards(): part = lax.all_to_all(part, 'z', 0, 0, tiled=True)]
where the time goes in v3:
time: 118 us; the launch traced here: 117 us
  waiting for transfers between devices  51.5 us (44%)
  blocking collectives  26 us (22%)
  starting transfers between devices  24 us (20%)
  Pallas kernels  12.2 us (10%)
  local copies, waits for them, and re-layouts  2.61 us (2%)
    all_to_all x1, blocking collectives, shards(): line = lax.all_to_all(own, 'z', 0, 0, tiled=True)  26 us
    ppermute x3, waiting for transfers between devices, shards(): lax.ppermute(line, 'y', [(s, (s + k) % ROWS_Y) for s in range(ROWS_Y)])  20.1 us
    ppermute x3, waiting for transfers between devices, shards(): lax.ppermute(parts[k], 'y', [(s, (s + k) % ROWS_Y) for s in range(ROWS_Y)])  17.4 us
    all_to_all x1, waiting for transfers between devices, shards(): part = lax.all_to_all(part, 'z', 0, 0, tiled=True)  14.1 us
    pallas_call x6, Pallas kernels, call(): pl.pallas_call(kernel, out_shape=[jax.ShapeDtypeStruct(s, d) for s, d in...  12.2 us
    ppermute x3, starting transfers between devices, shards(): lax.ppermute(parts[k], 'y', [(s, (s + k) % ROWS_Y) for s in range(ROWS_Y)])  9.2 us
    all_to_all x1, starting transfers between devices, shards(): part = lax.all_to_all(part, 'z', 0, 0, tiled=True)  5.37 us
    all_to_all x1, starting transfers between devices, shards(): feat = lax.all_to_all(feat, 'mp', 0, 0, tiled=True)  4.83 us
  transfers between devices with their start and end apart: 8, of which 5 were waited for; matrix products, arithmetic and copies ran while one was open for 0% of the time, Pallas kernels for 3%

profile of v3, /device:TPU:2, one launch (start us, length us, event | category | flops | bytes accessed | tf_op | source)
XLA Modules:
  0.0 117.1 jit_solution(15088677452897490034)
XLA Ops:
  0.6 2.2 %shard_map.102 = bf16[8,128,256]{2,1,0:T(8,128)(2,1)} custom-call(s32[1,128]{1,0:T(1,128)} %bitcast.10, bf16[512,128]{1,0:T(8,128)(2,1)} %key_hbm.1, bf16[512,128]{1,0:T(8,128)(2,1)} %value_hbm.1), custom_call_target="tpu_custom_call" | custom-call | flops 33554432 | bytes 1048576 | tf_op jit(solution)/shard_map/pallas_call | solution.py:248
  2.8 26.0 %all_to_all.15 = bf16[8,128,256]{2,1,0:T(8,128)(2,1)S(1)} all-to-all(bf16[8,128,256]{2,1,0:T(8,128)(2,1)} %shard_map.102), channel_id=1, replica_groups=mesh['y'=4,'z'=8,'mp'=8] {'z'}, dimensions={0} | all-to-all | bytes 1048576 | tf_op jit(solution)/shard_map/all_to_all | solution.py:289
  28.8 3.0 %collective-permute-start.2 = (bf16[1024,256]{1,0:T(8,128)(2,1)S(1)}, bf16[1024,256]{1,0:T(8,128)(2,1)S(1)}, u32[]{:S(2)}, u32[]{:S(2)}) collective-permute-start(bf16[1024,256]{1,0:T(8,128)(2,1)S(1)} %bitcast.6), channel_id=1, source_target_pairs={{0,192},{64,0},{128,64},{192,128},{1,193},{65,1},{129,65},{193,129... | collective-permute-start | bytes 1572872 | tf_op jit(solution)/shard_map/ppermute | solution.py:297
  31.8 0.6 collective-permute-start.1
  32.4 1.0 collective-permute-start
  33.4 0.7 copy-done.3
  34.1 1.2 %copy-done.1 = bf16[512,1024]{1,0:T(8,128)(2,1)S(1)} copy-done((bf16[512,1024]{1,0:T(8,128)(2,1)S(1)}, bf16[512,1024]{1,0:T(8,128)(2,1)}, u32[]{:S(2)}) %copy-start.1) | copy-done | bytes 1048600
  35.3 0.8 shard_map.101
  36.1 0.1 pad_add_fusion.pos_ref
  36.2 16.4 %collective-permute-done.2.kv3 = bf16[1024,256]{1,0:T(8,128)(2,1)S(1)} collective-permute-done((bf16[1024,256]{1,0:T(8,128)(2,1)S(1)}, bf16[1024,256]{1,0:T(8,128)(2,1)S(1)}, u32[]{:S(2)}, u32[]{:S(2)}) %collective-permute-start.2) | collective-permute-done | bytes 524320 | tf_op jit(solution)/shard_map/ppermute | solution.py:297
  52.6 3.7 %collective-permute-done.kv1 = bf16[1024,256]{1,0:T(8,128)(2,1)S(1)} collective-permute-done((bf16[1024,256]{1,0:T(8,128)(2,1)S(1)}, bf16[1024,256]{1,0:T(8,128)(2,1)S(1)}, u32[]{:S(2)}, u32[]{:S(2)}) %collective-permute-start) | collective-permute-done | bytes 524320 | tf_op jit(solution)/shard_map/ppermute | solution.py:297
  56.3 5.1 %shard_map.103 = (bf16[128,1024]{1,0:T(8,128)(2,1)S(1)}, bf16[128,1024]{1,0:T(8,128)(2,1)S(1)}, bf16[1024,256]{1,0:T(8,128)(2,1)S(1)}, bf16[1024,256]{1,0:T(8,12...) custom-call(s32[2]{0:T(128)S(1)} %pad_add_fusion.pos_ref, ...), custom_call_target="tpu_custom_call" | custom-call | flops 4026531840 | bytes 8388608 | tf_op jit(solution)/shard_map/pallas_call | solution.py:248
  61.4 0.7 copy-done.4
  62.1 1.5 %collective-permute-start.3 = (bf16[1024,256]{1,0:T(8,128)(2,1)}, bf16[1024,256]{1,0:T(8,128)(2,1)S(1)}, u32[]{:S(2)}, u32[]{:S(2)}) collective-permute-start(bf16[1024,256]{1,0:T(8,128)(2,1)} %get-tuple-element.31), channel_id=1, source_target_pairs={{0,64},{64,128},{128,192},{192,0},{1,65},{65,129},{129,193},{193,1... | collective-permute-start | bytes 1572872 | tf_op jit(solution)/shard_map/ppermute | solution.py:301
  63.7 7.6 %collective-permute-start.4 = (bf16[1024,256]{1,0:T(8,128)(2,1)}, bf16[1024,256]{1,0:T(8,128)(2,1)S(1)}, u32[]{:S(2)}, u32[]{:S(2)}) collective-permute-start(bf16[1024,256]{1,0:T(8,128)(2,1)} %get-tuple-element.32), channel_id=1, source_target_pairs={{0,128},{64,192},{128,0},{192,64},{1,129},{65,193},{129,1},{193,65... | collective-permute-start | bytes 1572872 | tf_op jit(solution)/shard_map/ppermute | solution.py:301
  71.3 0.0 collective-permute-start.5
  71.3 4.8 %all-to-all-start.1 = ((f32[8,8,128]{2,1,0:T(8,128)}), f32[8,8,128]{2,1,0:T(8,128)S(1)}, u32[]{:S(2)}, u32[]{:S(2)}) async-start(f32[8,8,128]{2,1,0:T(8,128)} %get-tuple-element.29), calls=%async_computation.1 | async-start | bytes 65536 | tf_op jit(solution)/shard_map/all_to_all | solution.py:302
  76.2 5.8 %collective-permute-done.3.in1 = bf16[1024,256]{1,0:T(8,128)(2,1)S(1)} collective-permute-done((bf16[1024,256]{1,0:T(8,128)(2,1)}, bf16[1024,256]{1,0:T(8,128)(2,1)S(1)}, u32[]{:S(2)}, u32[]{:S(2)}) %collective-permute-start.3) | collective-permute-done | bytes 524320 | tf_op jit(solution)/shard_map/ppermute | solution.py:301
  81.9 11.6 %collective-permute-done.4.in2 = bf16[1024,256]{1,0:T(8,128)(2,1)S(1)} collective-permute-done((bf16[1024,256]{1,0:T(8,128)(2,1)}, bf16[1024,256]{1,0:T(8,128)(2,1)S(1)}, u32[]{:S(2)}, u32[]{:S(2)}) %collective-permute-start.4) | collective-permute-done | bytes 524320 | tf_op jit(solution)/shard_map/ppermute | solution.py:301
  93.5 1.1 shard_map.105
  94.6 5.4 %all-to-all-start.2 = ((bf16[8,128,256]{2,1,0:T(8,128)(2,1)}), bf16[8,128,256]{2,1,0:T(8,128)(2,1)S(1)}, u32[]{:S(2)}, u32[]{:S(2)}) async-start(bf16[8,128,256]{2,1,0:T(8,128)(2,1)} %shard_map.105), calls=%async_computation.2 | async-start | bytes 1048576 | tf_op jit(solution)/shard_map/all_to_all | solution.py:307
  100.0 2.1 %shard_map.104 = (bf16[512,1024]{1,0:T(8,128)(2,1)}, bf16[512,1024]{1,0:T(8,128)(2,1)}) custom-call(s32[1,128]{1,0:T(1,128)S(1)} %bitcast.12, f32[128,128]{1,0:T(8,128)S(1)} %get-tuple-element.21.router_ref, bf16[128,1024]{1,0:T(8,128)(2,1)S(1)} %get-tuple-element.25.att_ref, bf16[128,1024]{1,0:T(8,128)(2,1)S(1)} %copy-done.5), custom_call_target="tpu_custom_call" | custom-call | flops 268435456 | bytes 3145728 | tf_op jit(solution)/shard_map/pallas_call | solution.py:248
  102.1 14.1 %all-to-all-done.2.part_ref = bf16[8,128,256]{2,1,0:T(8,128)(2,1)S(1)} async-done(((bf16[8,128,256]{2,1,0:T(8,128)(2,1)}), bf16[8,128,256]{2,1,0:T(8,128)(2,1)S(1)}, u32[]{:S(2)}, u32[]{:S(2)}) %all-to-all-start.2) | async-done | bytes 524320 | tf_op jit(solution)/shard_map/all_to_all | solution.py:307
  116.1 1.0 shard_map.106
  (12 shorter events, 0.0 us)
Async XLA Ops:
  0.6 32.8 %copy-start = (bf16[512,1024]{1,0:T(8,128)(2,1)S(1)}, bf16[512,1024]{1,0:T(8,128)(2,1)}, u32[]{:S(2)}) copy-start(bf16[512,1024]{1,0:T(8,128)(2,1)} %query_ref.1) | copy-start | bytes 3145732
  28.8 23.8 %collective-permute-start.2 = (bf16[1024,256]{1,0:T(8,128)(2,1)S(1)}, bf16[1024,256]{1,0:T(8,128)(2,1)S(1)}, u32[]{:S(2)}, u32[]{:S(2)}) collective-permute-start(bf16[1024,256]{1,0:T(8,128)(2,1)S(1)} %bitcast.6), channel_id=1, source_target_pairs={{0,192},{64,0},{128,64},{192,128},{1,193},{65,1},{129,65},{193,129... | collective-permute-start | bytes 1572872 | tf_op jit(solution)/shard_map/ppermute | solution.py:297
  31.8 20.8 %collective-permute-start.1 = (bf16[1024,256]{1,0:T(8,128)(2,1)S(1)}, bf16[1024,256]{1,0:T(8,128)(2,1)S(1)}, u32[]{:S(2)}, u32[]{:S(2)}) collective-permute-start(bf16[1024,256]{1,0:T(8,128)(2,1)S(1)} %bitcast.7), channel_id=1, source_target_pairs={{0,128},{64,192},{128,0},{192,64},{1,129},{65,193},{129,1},{193,65... | collective-permute-start | bytes 1572872 | tf_op jit(solution)/shard_map/ppermute | solution.py:297
  32.4 23.8 %collective-permute-start = (bf16[1024,256]{1,0:T(8,128)(2,1)S(1)}, bf16[1024,256]{1,0:T(8,128)(2,1)S(1)}, u32[]{:S(2)}, u32[]{:S(2)}) collective-permute-start(bf16[1024,256]{1,0:T(8,128)(2,1)S(1)} %bitcast.8), channel_id=1, source_target_pairs={{0,64},{64,128},{128,192},{192,0},{1,65},{65,129},{129,193},{193,1... | collective-permute-start | bytes 1572872 | tf_op jit(solution)/shard_map/ppermute | solution.py:297
  33.4 0.7 copy-start.3
  33.4 0.7 copy-start.2
  34.1 1.2 %copy-start.1 = (bf16[512,1024]{1,0:T(8,128)(2,1)S(1)}, bf16[512,1024]{1,0:T(8,128)(2,1)}, u32[]{:S(2)}) copy-start(bf16[512,1024]{1,0:T(8,128)(2,1)} %cot_ref.1) | copy-start | bytes 3145732
  61.4 0.7 copy-start.4
  62.1 19.8 %collective-permute-start.3 = (bf16[1024,256]{1,0:T(8,128)(2,1)}, bf16[1024,256]{1,0:T(8,128)(2,1)S(1)}, u32[]{:S(2)}, u32[]{:S(2)}) collective-permute-start(bf16[1024,256]{1,0:T(8,128)(2,1)} %get-tuple-element.31), channel_id=1, source_target_pairs={{0,64},{64,128},{128,192},{192,0},{1,65},{65,129},{129,193},{193,1... | collective-permute-start | bytes 1572872 | tf_op jit(solution)/shard_map/ppermute | solution.py:301
  63.7 29.9 %collective-permute-start.4 = (bf16[1024,256]{1,0:T(8,128)(2,1)}, bf16[1024,256]{1,0:T(8,128)(2,1)S(1)}, u32[]{:S(2)}, u32[]{:S(2)}) collective-permute-start(bf16[1024,256]{1,0:T(8,128)(2,1)} %get-tuple-element.32), channel_id=1, source_target_pairs={{0,128},{64,192},{128,0},{192,64},{1,129},{65,193},{129,1},{193,65... | collective-permute-start | bytes 1572872 | tf_op jit(solution)/shard_map/ppermute | solution.py:301
  71.3 22.2 %collective-permute-start.5 = (bf16[1024,256]{1,0:T(8,128)(2,1)}, bf16[1024,256]{1,0:T(8,128)(2,1)S(1)}, u32[]{:S(2)}, u32[]{:S(2)}) collective-permute-start(bf16[1024,256]{1,0:T(8,128)(2,1)} %get-tuple-element.33), channel_id=1, source_target_pairs={{0,192},{64,0},{128,64},{192,128},{1,193},{65,1},{129,65},{193,129... | collective-permute-start | bytes 1572872 | tf_op jit(solution)/shard_map/ppermute | solution.py:301
  71.3 23.3 %all-to-all-start.1 = ((f32[8,8,128]{2,1,0:T(8,128)}), f32[8,8,128]{2,1,0:T(8,128)S(1)}, u32[]{:S(2)}, u32[]{:S(2)}) async-start(f32[8,8,128]{2,1,0:T(8,128)} %get-tuple-element.29), calls=%async_computation.1 | async-start | bytes 65536 | tf_op jit(solution)/shard_map/all_to_all | solution.py:302
  94.6 5.4 %copy-start.5 = (bf16[128,1024]{1,0:T(8,128)(2,1)S(1)}, bf16[128,1024]{1,0:T(8,128)(2,1)}, u32[]{:S(2)}) copy-start(bf16[128,1024]{1,0:T(8,128)(2,1)} %copy-done.4) | copy-start | bytes 786436
  94.6 21.5 %all-to-all-start.2 = ((bf16[8,128,256]{2,1,0:T(8,128)(2,1)}), bf16[8,128,256]{2,1,0:T(8,128)(2,1)S(1)}, u32[]{:S(2)}, u32[]{:S(2)}) async-start(bf16[8,128,256]{2,1,0:T(8,128)(2,1)} %shard_map.105), calls=%async_computation.2 | async-start | bytes 1048576 | tf_op jit(solution)/shard_map/all_to_all | solution.py:307
